TPU v7x, 128 devices: a whole 4x4x4 slice. The times are simulated.
128 devices in a mesh: event: 8 (over z, core), slab: 16 (over y, x).
Axes of the slice: x: 4, y: 4, z: 4, core: 2. Of those that a mesh axis runs over, the one named last changes fastest.
Arguments:
- wave_prev: float32 [8, 512, 128, 128], P('event', 'slab'), may hold values from -6 to 6
- wave_now: float32 [8, 512, 128, 128], P('event', 'slab'), may hold values from -6 to 6
- adjoint: float32 [8, 4, 512, 128, 128], P('event', None, 'slab'), may hold values from -6 to 6
- background: float32 [8, 512, 128, 128], P('event', 'slab'), may hold values from 0.02 to 0.12
- coeffs_x: float32 [8, 512, 9], P('event', 'slab'), may hold values from -2 to 2
- stiff_y: float32 [128, 128], replicated, may hold values from -0.5 to 0.5
- stiff_z: float32 [128, 128], replicated, may hold values from -0.5 to 0.5
- interp_y: bfloat16 [16, 32], replicated, may hold values from -1.5 to 1.5
- interp_z: bfloat16 [128, 128], replicated, may hold values from -0.5 to 0.5
- model: bfloat16 [2048, 16, 128], P(('event', 'slab')), may hold values from -1.796875 to 1.796875
- block_index: int32 [8, 512, 4], P('event', 'slab'), may hold values from 0 to 2047, as said below
- live_count: int32 [8, 16], P('event', 'slab'), may hold values from 1 to 128, as said below
Outputs:
- wave_last: float32 [8, 512, 128, 128], P('event', 'slab')
- model_gradient: float32 [2048, 16, 128], P(('event', 'slab'))
Inputs may be any that keep to these rules, and one draw needn't show every extreme that they name: `block_index`: within one slab of one event, at most 2 tiles name blocks owned by one device, and some device owns exactly 2 of them. `live_count`: some slab has all 128 tiles live.
All inputs are finite; a program needn't handle non-finite values.
Results may differ from a plain program's by a relative error of at most 0.0029.
Values may be sent and summed in bfloat16 or wider, within the bound.
A program may use at most 128 MiB of HBM per device.

v0:
```python
import jax
import jax.numpy as jnp
from jax import lax
from jax.sharding import PartitionSpec as P

HIGH = lax.Precision.HIGHEST


def padded_2(value, sides, width):
    for axis, dim in sides:
        devices, length = (lax.axis_size(axis), value.shape[dim])
        up = [(i, (i + 1) % devices) for i in range(devices - 1)]
        down = [(j, i) for i, j in up]
        last = lax.slice_in_dim(value, length - width, length, axis=dim)
        initial = lax.slice_in_dim(value, 0, width, axis=dim)
        before = lax.ppermute(last, axis, up)
        after = lax.ppermute(initial, axis, down)
        value = jnp.concatenate([before, value, after], axis=dim)
    return value


def cut_along(value, dim, devices):
    dims = value.shape
    tiles = value.reshape(*dims[:dim], devices, dims[dim] // devices, *dims[dim + 1 :])
    return jnp.moveaxis(tiles, dim, 0)


def joined_along(tiles, dim):
    dims = list(tiles.shape[1:])
    dims[dim] *= tiles.shape[0]
    return jnp.moveaxis(tiles, 0, dim).reshape(dims)


def one_exchange(value, axis, axes, splits, concats):
    sizes = [lax.axis_size(a) for a in axes]
    tiles = cut_along(value, splits[0], sizes[0])
    tiles = jnp.moveaxis(cut_along(tiles, splits[1] + 1, sizes[1]), 0, 1)
    inside = tiles.shape[2:]
    tiles = tiles.reshape(-1, *inside)
    tiles = lax.all_to_all(tiles, axis, split_axis=0, concat_axis=0, tiled=True)
    tiles = joined_along(tiles.reshape(*sizes, *inside), concats[0] + 1)
    return joined_along(tiles, concats[1])


def stencil_sum(padded, wavefield, coeffs, stiff_y, stiff_z, half_width):
    n_planes = wavefield.shape[0]
    result = jnp.einsum("yw,xwz->xyz", stiff_y, wavefield, precision=HIGH)
    result = result + jnp.einsum("xyw,zw->xyz", wavefield, stiff_z, precision=HIGH)
    for offset in range(2 * half_width + 1):
        result = result + coeffs[:, offset][:, None, None] * padded[offset : offset + n_planes]
    return result


def stiffness(wavefield, coeffs, stiff_y, stiff_z):
    half_width = (coeffs.shape[-1] - 1) // 2
    padded = padded_2(wavefield, (("slab", 0),), half_width)
    return stencil_sum(padded, wavefield, coeffs, stiff_y, stiff_z, half_width)


def interpolate(blocks, interp_y, interp_z):
    n_tiles = blocks.shape[0]
    along_z = jnp.dot(
        blocks.reshape(-1, blocks.shape[2]), interp_z, preferred_element_type=jnp.float32
    )
    along_z = along_z.reshape(n_tiles, blocks.shape[1], -1)
    return jnp.einsum("by,tbz->tyz", interp_y.astype(jnp.float32), along_z, precision=HIGH)


def transpose_interp(kernel_low, interp_y, interp_z, n_tiles):
    rows_tile = interp_y.shape[1]
    back_z = jnp.dot(
        kernel_low.reshape(-1, kernel_low.shape[2]), interp_z.T, preferred_element_type=jnp.float32
    )
    back_z = back_z.reshape(n_tiles, rows_tile, -1)
    return jnp.einsum("by,tyc->tbc", interp_y.astype(jnp.float32), back_z, precision=HIGH)


def shards(
    wave_prev,
    wave_now,
    adjoint,
    background,
    coeffs_x,
    stiff_y,
    stiff_z,
    interp_y,
    interp_z,
    model,
    block_index,
    live_count,
):
    n_event = lax.axis_size("event")
    n_slab = lax.axis_size("slab")
    devices = n_event * n_slab
    blk_dev, rows_y, rows_z = model.shape
    n_planes, mesh_y, mesh_z = wave_now.shape[1:]
    tiles_y = block_index.shape[2]
    n_tiles = n_planes * tiles_y
    rows_tile = mesh_y // tiles_y
    capacity = max(1, 2 * n_tiles // devices)
    block_ids = block_index[0].reshape(n_tiles)
    owners = block_ids // blk_dev
    local_ids = block_ids % blk_dev
    positions = jnp.arange(n_tiles, dtype=jnp.int32)
    same_owner = (owners[:, None] == owners[None, :]) & (positions[None, :] < positions[:, None])
    slot_rank = jnp.sum(same_owner.astype(jnp.int32), axis=1)
    slot_ids = owners * capacity + slot_rank
    requests = (
        jnp.zeros((devices * capacity,), jnp.int32)
        .at[slot_ids]
        .set(local_ids)
        .reshape(devices, capacity)
    )
    asked_ids = one_exchange(
        requests.reshape(n_event, n_slab, capacity),
        ("event", "slab"),
        ("event", "slab"),
        (0, 1),
        (0, 1),
    )
    blocks_found = model[asked_ids]
    fetched = one_exchange(blocks_found, ("event", "slab"), ("event", "slab"), (0, 1), (0, 1))
    fetched = fetched.reshape(devices * capacity, rows_y, rows_z)
    asked_ids = asked_ids.reshape(devices * capacity)
    blocks = fetched[slot_ids]
    perturb = interpolate(blocks, interp_y, interp_z).reshape(n_planes, mesh_y, mesh_z)
    tile_num = (
        jnp.arange(n_planes, dtype=jnp.int32)[:, None] * tiles_y
        + jnp.arange(tiles_y, dtype=jnp.int32)[None, :]
    )
    alive = tile_num < live_count[0, 0]
    alive_rows = jnp.repeat(alive, rows_tile, axis=1)[:, :, None]
    background_now = background[0]
    speed_sq = background_now * jnp.exp(jnp.where(alive_rows, perturb, jnp.zeros_like(perturb)))
    coeffs = coeffs_x[0]
    prev_w = wave_prev[0]
    now_w = wave_now[0]
    kernel = jnp.zeros_like(now_w)
    n_steps = adjoint.shape[1]
    for time_step in range(n_steps):
        stiff_u = stiffness(now_w, coeffs, stiff_y, stiff_z)
        kernel = kernel - adjoint[0, time_step] * speed_sq * stiff_u
        prev_w, now_w = (now_w, 2.0 * now_w - prev_w - speed_sq * stiff_u)
    gradients = transpose_interp(kernel.astype(jnp.bfloat16), interp_y, interp_z, n_tiles)
    gradients = gradients * alive.reshape(-1)[:, None, None].astype(jnp.float32)
    outgoing = (
        jnp.zeros((devices * capacity, rows_y, rows_z), jnp.float32).at[slot_ids].set(gradients)
    )
    received = one_exchange(
        outgoing.reshape(n_event, n_slab, capacity, rows_y, rows_z),
        ("event", "slab"),
        ("event", "slab"),
        (0, 1),
        (0, 1),
    )
    received = received.reshape(devices * capacity, rows_y * rows_z)
    one_hot = (asked_ids[None, :] == jnp.arange(blk_dev, dtype=jnp.int32)[:, None]).astype(
        jnp.float32
    )
    model_gradient = jnp.dot(one_hot, received, precision=HIGH, preferred_element_type=jnp.float32)
    return (now_w[None], model_gradient.reshape(blk_dev, rows_y, rows_z))


def solution(mesh):
    return jax.shard_map(
        shards,
        mesh=mesh,
        in_specs=(
            P("event", "slab", None, None),
            P("event", "slab", None, None),
            P("event", None, "slab", None, None),
            P("event", "slab", None, None),
            P("event", "slab", None),
            P(),
            P(),
            P(),
            P(),
            P(("event", "slab"), None, None),
            P("event", "slab", None),
            P("event", "slab"),
        ),
        out_specs=(P("event", "slab", None, None), P(("event", "slab"), None, None)),
        check_vma=False,
    )
```

profile of v0, /device:TPU:1, one launch (start us, length us, event | category | flops | bytes accessed | tf_op | source)
XLA Modules:
  0.0 197.8 jit_solution(10988344295521589363)
XLA Ops:
  3.6 20.9 %all_to_all.15 = s32[128,1,1,2]{3,2,1,0:T(1,128)S(1)} all-to-all(s32[128,1,1,2]{3,2,1,0:T(1,128)S(1)} %bitcast.213), channel_id=1, replica_groups=mesh['event'=8,'slab'=16] {'event','slab'}, dimensions={0} | all-to-all | bytes 2048 | tf_op jit(solution)/shard_map/all_to_all | solution.py:40
  24.6 2.7 %gather_fusion = bf16[256,16,128]{2,1,0:T(8,128)(2,1)} fusion(bf16[16,16,128]{2,1,0:T(8,128)(2,1)} %param.21, s32[1024]{0:T(1024)S(1)} %pad_clamp_fusion.1), kind=kCustom, calls=%fused_computation | custom fusion | bytes 2098176 | tf_op jit(solution)/shard_map/gather | solution.py:121
  27.4 4.5 %all-to-all-start.1 = ((bf16[128,1,1,2,16,128]{5,4,3,2,1,0:T(8,128)(2,1)}), bf16[128,1,1,2,16,128]{5,4,3,2,1,0:T(8,128)(2,1)S(1)}, u32[]{:S(2)}, u32[]{:S(2)}) async-start(bf16[128,1,1,2,16,128]{5,4,3,2,1,0:T(8,128)(2,1)} %bitcast.16), calls=%async_computation.1 | async-start | bytes 2097152 | tf_op jit(solution)/shard_map/all_to_all | solution.py:40
  32.7 4.0 %collective-permute-start = (f32[4,128,128]{2,1,0:T(8,128)}, f32[4,128,128]{2,1,0:T(8,128)}, u32[]{:S(2)}, u32[]{:S(2)}) collective-permute-start(f32[4,128,128]{2,1,0:T(8,128)} %get-tuple-element.20), channel_id=1, source_target_pairs={{0,1},{1,2},{2,3},{3,4},{4,5},{5,6},{6,7},{7,8},{8,9},{9,10},{10,1... | collective-permute-start | bytes 786440 | tf_op jit(solution)/shard_map/ppermute | solution.py:16
  42.7 1.6 slice_bitcast_fusion.10
  44.3 3.2 %fusion.106 = f32[32,128,128]{2,1,0:T(8,128)} fusion(f32[128,128]{1,0:T(8,128)S(1)} %copy-done, f32[1,32,128,128]{3,2,1,0:T(8,128)S(1)} %copy-done.1), kind=kOutput, calls=%fused_computation.184 | convolution fusion | flops 805306368 | bytes 4259840 | tf_op jit(solution)/shard_map/xyw,zw->xyz/dot_general | solution.py:48
  47.5 3.6 %all-to-all-done.1 = bf16[128,1,1,2,16,128]{5,4,3,2,1,0:T(8,128)(2,1)S(1)} async-done(((bf16[128,1,1,2,16,128]{5,4,3,2,1,0:T(8,128)(2,1)}), bf16[128,1,1,2,16,128]{5,4,3,2,1,0:T(8,128)(2,1)S(1)}, u32[]{:S(2)}, u32[]{:S(2)}) %all-to-all-start.1) | async-done | bytes 1048608 | tf_op jit(solution)/shard_map/all_to_all | solution.py:40
  51.1 1.5 gather_fusion.1
  52.6 1.3 fusion.118
  54.0 2.3 %fusion.125 = f32[128,128,32]{1,2,0:T(8,128)} fusion(f32[128,16,128]{2,1,0:T(8,128)S(1)} %fusion.118, bf16[16,32]{1,0:T(8,128)(2,1)S(1)} %copy-done.7), kind=kOutput, calls=%fused_computation.209 | convolution fusion | flops 100663296 | bytes 3146752 | tf_op jit(solution)/shard_map/by,tbz->tyz/dot_general | solution.py:66
  56.4 9.9 %fusion.101 = (f32[32,128,128]{2,1,0:T(8,128)S(1)}, f32[32,128,128]{2,1,0:T(8,128)}, f32[32,128,128]{2,1,0:T(8,128)}) fusion(f32[1,32,128,128]{3,2,1,0:T(8,128)} %param.12, f32[1,32,128,128]{3,2,1,0:T(8,128)S(1)} %copy-done.1, f32[32,128,128]{2,1,0:T(8,128)} %bitcast.209, pred[32,128]{1,0:T(8,128)(4,1)S(1)} %copy-done.9, f32[1,32,128,128]{3,2,1,0:T(8,128)} %param.15, ...), kind=kOutput, calls=%fused_computation.172 | convolution fusion | flops 822607872 | bytes 21570048 | tf_op jit(solution)/shard_map/yw,xwz->xyz/dot_general | solution.py:47
  66.4 2.6 %collective-permute-start.2 = (f32[4,128,128]{2,1,0:T(8,128)S(1)}, f32[4,128,128]{2,1,0:T(8,128)S(1)}, u32[]{:S(2)}, u32[]{:S(2)}) collective-permute-start(f32[4,128,128]{2,1,0:T(8,128)S(1)} %get-tuple-element.18), channel_id=1, source_target_pairs={{0,1},{1,2},{2,3},{3,4},{4,5},{5,6},{6,7},{7,8},{8,9},{9,10},{10,1... | collective-permute-start | bytes 786440 | tf_op jit(solution)/shard_map/ppermute | solution.py:16
  69.0 1.4 collective-permute-start.3
  70.5 2.0 %fusion.112 = f32[32,128,128]{1,2,0:T(8,128)S(1)} fusion(f32[32,128,128]{2,1,0:T(8,128)S(1)} %get-tuple-element.10, f32[128,128]{1,0:T(8,128)S(1)} %copy-done.5), kind=kOutput, calls=%fused_computation.190 | convolution fusion | flops 805306368 | bytes 4259840 | tf_op jit(solution)/shard_map/yw,xwz->xyz/dot_general | solution.py:47
  73.6 4.0 %collective-permute-done.3 = f32[4,128,128]{2,1,0:T(8,128)S(1)} collective-permute-done((f32[4,128,128]{2,1,0:T(8,128)S(1)}, f32[4,128,128]{2,1,0:T(8,128)S(1)}, u32[]{:S(2)}, u32[]{:S(2)}) %collective-permute-start.3) | collective-permute-done | bytes 262176 | tf_op jit(solution)/shard_map/ppermute | solution.py:17
  77.6 5.9 %multiply_subtract_fusion.1 = (f32[32,128,128]{2,1,0:T(8,128)S(1)}, f32[32,128,128]{2,1,0:T(8,128)}) fusion(f32[32,128,128]{2,1,0:T(8,128)S(1)} %copy-done.28, f32[32,128,128]{2,1,0:T(8,128)S(1)} %get-tuple-element.10, f32[1,32,128,128]{3,2,1,0:T(8,128)S(1)} %copy-done.1, f32[4,128,128]{2,1,0:T(8,128)S(1)} %collective-permute-done.3, ...), kind=kOutput, calls=%fused_computation.175 | convolution fusion | flops 821559296 | bytes 15274496 | tf_op jit(solution)/shard_map/xyw,zw->xyz/dot_general | solution.py:48
  83.6 2.3 %collective-permute-start.4 = (f32[4,128,128]{2,1,0:T(8,128)S(1)}, f32[4,128,128]{2,1,0:T(8,128)S(1)}, u32[]{:S(2)}, u32[]{:S(2)}) collective-permute-start(f32[4,128,128]{2,1,0:T(8,128)S(1)} %get-tuple-element.16), channel_id=1, source_target_pairs={{0,1},{1,2},{2,3},{3,4},{4,5},{5,6},{6,7},{7,8},{8,9},{9,10},{10,1... | collective-permute-start | bytes 786440 | tf_op jit(solution)/shard_map/ppermute | solution.py:16
  85.9 1.6 collective-permute-start.5
  87.5 2.0 %fusion.110 = f32[32,128,128]{1,2,0:T(8,128)S(1)} fusion(f32[32,128,128]{2,1,0:T(8,128)S(1)} %get-tuple-element.36, f32[128,128]{1,0:T(8,128)S(1)} %copy-done.5), kind=kOutput, calls=%fused_computation.188 | convolution fusion | flops 805306368 | bytes 4259840 | tf_op jit(solution)/shard_map/yw,xwz->xyz/dot_general | solution.py:47
  89.5 3.6 %collective-permute-done.5 = f32[4,128,128]{2,1,0:T(8,128)S(1)} collective-permute-done((f32[4,128,128]{2,1,0:T(8,128)S(1)}, f32[4,128,128]{2,1,0:T(8,128)S(1)}, u32[]{:S(2)}, u32[]{:S(2)}) %collective-permute-start.5) | collective-permute-done | bytes 262176 | tf_op jit(solution)/shard_map/ppermute | solution.py:17
  93.1 5.6 %multiply_subtract_fusion = (f32[32,128,128]{2,1,0:T(8,128)S(1)}, f32[32,128,128]{2,1,0:T(8,128)}) fusion(f32[32,128,128]{2,1,0:T(8,128)S(1)} %copy-done.29, f32[32,128,128]{2,1,0:T(8,128)S(1)} %get-tuple-element.10, f32[32,128,128]{2,1,0:T(8,128)S(1)} %get-tuple-element.36, f32[4,128,128]{2,1,0:T(8,128)S(1)} %collective-permute-done.5, ...), kind=kOutput, calls=%fused_computation.174 | convolution fusion | flops 821559296 | bytes 15274496 | tf_op jit(solution)/shard_map/xyw,zw->xyz/dot_general | solution.py:48
  98.8 7.6 %collective-permute-start.6 = (f32[4,128,128]{2,1,0:T(8,128)S(1)}, f32[4,128,128]{2,1,0:T(8,128)S(1)}, u32[]{:S(2)}, u32[]{:S(2)}) collective-permute-start(f32[4,128,128]{2,1,0:T(8,128)S(1)} %get-tuple-element.14), channel_id=1, source_target_pairs={{0,1},{1,2},{2,3},{3,4},{4,5},{5,6},{6,7},{7,8},{8,9},{9,10},{10,1... | collective-permute-start | bytes 786440 | tf_op jit(solution)/shard_map/ppermute | solution.py:16
  106.4 1.4 collective-permute-start.7
  107.9 3.4 %fusion.108 = f32[32,128,128]{1,2,0:T(8,128)} fusion(f32[32,128,128]{2,1,0:T(8,128)S(1)} %get-tuple-element.38, f32[128,128]{1,0:T(8,128)S(1)} %copy-done.5), kind=kOutput, calls=%fused_computation.186 | convolution fusion | flops 805306368 | bytes 4259840 | tf_op jit(solution)/shard_map/yw,xwz->xyz/dot_general | solution.py:47
  111.2 2.4 %collective-permute-done.7 = f32[4,128,128]{2,1,0:T(8,128)S(1)} collective-permute-done((f32[4,128,128]{2,1,0:T(8,128)S(1)}, f32[4,128,128]{2,1,0:T(8,128)S(1)}, u32[]{:S(2)}, u32[]{:S(2)}) %collective-permute-start.7) | collective-permute-done | bytes 262176 | tf_op jit(solution)/shard_map/ppermute | solution.py:17
  114.5 18.1 %fusion.94 = (bf16[32,128,128]{2,1,0:T(8,128)(2,1)S(1)}, f32[1,32,128,128]{3,2,1,0:T(8,128)}) fusion(f32[32,128,128]{2,1,0:T(8,128)} %get-tuple-element.11, f32[32,128,128]{2,1,0:T(8,128)} %get-tuple-element.39, f32[32,128,128]{2,1,0:T(8,128)} %get-tuple-element.37, f32[32,128,128]{2,1,0:T(8,128)} %get-tuple-element.35, ...), kind=kOutput, calls=%fused_computation.156 | convolution fusion | flops 828375040 | bytes 28902528 | tf_op jit(solution)/shard_map/xyw,zw->xyz/dot_general | solution.py:48
  134.0 1.5 broadcast_in_dim.38
  135.5 13.6 %scatter_fusion = f32[256,16,128]{2,1,0:T(8,128)} fusion(f32[256,16,128]{2,1,0:T(8,128)} %broadcast_in_dim.38, s32[128]{0:T(128)S(1)} %copy-done.11, f32[128,16,128]{2,1,0:T(8,128)S(1)} %fusion.102), kind=kCustom, calls=%fused_computation.3 | custom fusion | bytes 3146240 | tf_op jit(solution)/shard_map/scatter | solution.py:147
  149.1 13.0 %all-to-all-start.2 = ((f32[128,1,1,2,16,128]{5,4,3,2,1,0:T(8,128)}), f32[128,1,1,2,16,128]{5,4,3,2,1,0:T(8,128)S(1)}, u32[]{:S(2)}, u32[]{:S(2)}) async-start(f32[128,1,1,2,16,128]{5,4,3,2,1,0:T(8,128)} %bitcast.52), calls=%async_computation.2 | async-start | bytes 4194304 | tf_op jit(solution)/shard_map/all_to_all | solution.py:40
  162.3 29.6 %all-to-all-done.2 = f32[128,1,1,2,16,128]{5,4,3,2,1,0:T(8,128)S(1)} async-done(((f32[128,1,1,2,16,128]{5,4,3,2,1,0:T(8,128)}), f32[128,1,1,2,16,128]{5,4,3,2,1,0:T(8,128)S(1)}, u32[]{:S(2)}, u32[]{:S(2)}) %all-to-all-start.2) | async-done | bytes 2097184 | tf_op jit(solution)/shard_map/all_to_all | solution.py:40
  191.8 2.2 %copy.38 = f32[32,8,16,128]{3,1,2,0:T(8,128)} copy(f32[32,8,16,128]{3,2,1,0:T(8,128)S(1)} %bitcast.204) | data formatting | bytes 4194304
  194.1 1.9 copy.32
  (93 shorter events, 14.6 us)
Async XLA Ops:
  0.6 43.7 %copy-start = (f32[128,128]{1,0:T(8,128)S(1)}, f32[128,128]{1,0:T(8,128)}, u32[]{:S(2)}) copy-start(f32[128,128]{1,0:T(8,128)} %param.18) | copy-start | bytes 196612
  24.6 7.3 %copy-start.1 = (f32[1,32,128,128]{3,2,1,0:T(8,128)S(1)}, f32[1,32,128,128]{3,2,1,0:T(8,128)}, u32[]{:S(2)}) copy-start(f32[1,32,128,128]{3,2,1,0:T(8,128)} %param.13) | copy-start | bytes 6291460
  27.4 11.2 %copy-start.8 = (f32[1,32,9]{1,0,2:T(1,128)S(1)}, f32[1,32,9]{1,0,2:T(1,128)}, u32[]{:S(2)}) copy-start(f32[1,32,9]{1,0,2:T(1,128)} %param.16) | copy-start | bytes 3460
  27.4 23.7 %all-to-all-start.1 = ((bf16[128,1,1,2,16,128]{5,4,3,2,1,0:T(8,128)(2,1)}), bf16[128,1,1,2,16,128]{5,4,3,2,1,0:T(8,128)(2,1)S(1)}, u32[]{:S(2)}, u32[]{:S(2)}) async-start(bf16[128,1,1,2,16,128]{5,4,3,2,1,0:T(8,128)(2,1)} %bitcast.16), calls=%async_computation.1 | async-start | bytes 2097152 | tf_op jit(solution)/shard_map/all_to_all | solution.py:40
  32.7 23.6 %collective-permute-start = (f32[4,128,128]{2,1,0:T(8,128)}, f32[4,128,128]{2,1,0:T(8,128)}, u32[]{:S(2)}, u32[]{:S(2)}) collective-permute-start(f32[4,128,128]{2,1,0:T(8,128)} %get-tuple-element.20), channel_id=1, source_target_pairs={{0,1},{1,2},{2,3},{3,4},{4,5},{5,6},{6,7},{7,8},{8,9},{9,10},{10,1... | collective-permute-start | bytes 786440 | tf_op jit(solution)/shard_map/ppermute | solution.py:16
  36.7 19.6 %collective-permute-start.1 = (f32[4,128,128]{2,1,0:T(8,128)S(1)}, f32[4,128,128]{2,1,0:T(8,128)}, u32[]{:S(2)}, u32[]{:S(2)}) collective-permute-start(f32[4,128,128]{2,1,0:T(8,128)S(1)} %get-tuple-element.21), channel_id=1, source_target_pairs={{1,0},{2,1},{3,2},{4,3},{5,4},{6,5},{7,6},{8,7},{9,8},{10,9},{11,1... | collective-permute-start | bytes 786440 | tf_op jit(solution)/shard_map/ppermute | solution.py:17
  47.5 6.4 %copy-start.7 = (bf16[16,32]{1,0:T(8,128)(2,1)S(1)}, bf16[16,32]{1,0:T(8,128)(2,1)}, u32[]{:S(2)}) copy-start(bf16[16,32]{1,0:T(8,128)(2,1)} %param.19) | copy-start | bytes 3076
  52.6 3.8 %copy-start.14 = (f32[32]{0:T(128)S(1)}, f32[32]{0:T(128)}, u32[]{:S(2)}) copy-start(f32[32]{0:T(128)} %get-tuple-element.25) | copy-start | bytes 388
  52.6 3.8 %copy-start.16 = (f32[32]{0:T(128)S(1)}, f32[32]{0:T(128)}, u32[]{:S(2)}) copy-start(f32[32]{0:T(128)} %get-tuple-element.26) | copy-start | bytes 388
  52.6 3.8 %copy-start.18 = (f32[32]{0:T(128)S(1)}, f32[32]{0:T(128)}, u32[]{:S(2)}) copy-start(f32[32]{0:T(128)} %get-tuple-element.27) | copy-start | bytes 388
  52.6 3.8 %copy-start.20 = (f32[32]{0:T(128)S(1)}, f32[32]{0:T(128)}, u32[]{:S(2)}) copy-start(f32[32]{0:T(128)} %get-tuple-element.28) | copy-start | bytes 388
  52.6 3.8 %copy-start.22 = (f32[32]{0:T(128)S(1)}, f32[32]{0:T(128)}, u32[]{:S(2)}) copy-start(f32[32]{0:T(128)} %get-tuple-element.29) | copy-start | bytes 388
  52.6 3.8 %copy-start.24 = (f32[32]{0:T(128)S(1)}, f32[32]{0:T(128)}, u32[]{:S(2)}) copy-start(f32[32]{0:T(128)} %get-tuple-element.30) | copy-start | bytes 388
  66.4 7.2 %collective-permute-start.2 = (f32[4,128,128]{2,1,0:T(8,128)S(1)}, f32[4,128,128]{2,1,0:T(8,128)S(1)}, u32[]{:S(2)}, u32[]{:S(2)}) collective-permute-start(f32[4,128,128]{2,1,0:T(8,128)S(1)} %get-tuple-element.18), channel_id=1, source_target_pairs={{0,1},{1,2},{2,3},{3,4},{4,5},{5,6},{6,7},{7,8},{8,9},{9,10},{10,1... | collective-permute-start | bytes 786440 | tf_op jit(solution)/shard_map/ppermute | solution.py:16
  69.0 8.6 %copy-start.28 = (f32[32,128,128]{2,1,0:T(8,128)S(1)}, f32[32,128,128]{2,1,0:T(8,128)}, u32[]{:S(2)}) copy-start(f32[32,128,128]{2,1,0:T(8,128)} %get-tuple-element.11) | copy-start | bytes 6291460
  69.0 8.6 %collective-permute-start.3 = (f32[4,128,128]{2,1,0:T(8,128)S(1)}, f32[4,128,128]{2,1,0:T(8,128)S(1)}, u32[]{:S(2)}, u32[]{:S(2)}) collective-permute-start(f32[4,128,128]{2,1,0:T(8,128)S(1)} %get-tuple-element.19), channel_id=1, source_target_pairs={{1,0},{2,1},{3,2},{4,3},{5,4},{6,5},{7,6},{8,7},{9,8},{10,9},{11,1... | collective-permute-start | bytes 786440 | tf_op jit(solution)/shard_map/ppermute | solution.py:17
  83.5 9.6 %copy-start.2 = (f32[32,128,128]{2,1,0:T(8,128)}, f32[32,128,128]{2,1,0:T(8,128)S(1)}, u32[]{:S(2)}) copy-start(f32[32,128,128]{2,1,0:T(8,128)S(1)} %get-tuple-element.36) | copy-start | bytes 6291460
  83.6 5.9 %collective-permute-start.4 = (f32[4,128,128]{2,1,0:T(8,128)S(1)}, f32[4,128,128]{2,1,0:T(8,128)S(1)}, u32[]{:S(2)}, u32[]{:S(2)}) collective-permute-start(f32[4,128,128]{2,1,0:T(8,128)S(1)} %get-tuple-element.16), channel_id=1, source_target_pairs={{0,1},{1,2},{2,3},{3,4},{4,5},{5,6},{6,7},{7,8},{8,9},{9,10},{10,1... | collective-permute-start | bytes 786440 | tf_op jit(solution)/shard_map/ppermute | solution.py:16
  85.8 7.3 %copy-start.29 = (f32[32,128,128]{2,1,0:T(8,128)S(1)}, f32[32,128,128]{2,1,0:T(8,128)}, u32[]{:S(2)}) copy-start(f32[32,128,128]{2,1,0:T(8,128)} %get-tuple-element.11) | copy-start | bytes 6291460
  85.9 7.2 %collective-permute-start.5 = (f32[4,128,128]{2,1,0:T(8,128)S(1)}, f32[4,128,128]{2,1,0:T(8,128)S(1)}, u32[]{:S(2)}, u32[]{:S(2)}) collective-permute-start(f32[4,128,128]{2,1,0:T(8,128)S(1)} %get-tuple-element.17), channel_id=1, source_target_pairs={{1,0},{2,1},{3,2},{4,3},{5,4},{6,5},{7,6},{8,7},{9,8},{10,9},{11,1... | collective-permute-start | bytes 786440 | tf_op jit(solution)/shard_map/ppermute | solution.py:17
  98.8 12.5 %copy-start.4 = (f32[32,128,128]{2,1,0:T(8,128)}, f32[32,128,128]{2,1,0:T(8,128)S(1)}, u32[]{:S(2)}) copy-start(f32[32,128,128]{2,1,0:T(8,128)S(1)} %get-tuple-element.38) | copy-start | bytes 6291460
  98.8 12.4 %collective-permute-start.6 = (f32[4,128,128]{2,1,0:T(8,128)S(1)}, f32[4,128,128]{2,1,0:T(8,128)S(1)}, u32[]{:S(2)}, u32[]{:S(2)}) collective-permute-start(f32[4,128,128]{2,1,0:T(8,128)S(1)} %get-tuple-element.14), channel_id=1, source_target_pairs={{0,1},{1,2},{2,3},{3,4},{4,5},{5,6},{6,7},{7,8},{8,9},{9,10},{10,1... | collective-permute-start | bytes 786440 | tf_op jit(solution)/shard_map/ppermute | solution.py:16
  106.4 8.0 %copy-start.3 = (f32[32,128,128]{2,1,0:T(8,128)S(1)}, f32[32,128,128]{2,1,0:T(8,128)}, u32[]{:S(2)}) copy-start(f32[32,128,128]{2,1,0:T(8,128)} %copy-done.2) | copy-start | bytes 6291460
  106.4 8.0 %copy-start.15 = (f32[32]{0:T(128)S(1)}, f32[32]{0:T(128)}, u32[]{:S(2)}) copy-start(f32[32]{0:T(128)} %get-tuple-element.25) | copy-start | bytes 388
  106.4 8.0 %copy-start.17 = (f32[32]{0:T(128)S(1)}, f32[32]{0:T(128)}, u32[]{:S(2)}) copy-start(f32[32]{0:T(128)} %get-tuple-element.26) | copy-start | bytes 388
  106.4 8.0 %copy-start.19 = (f32[32]{0:T(128)S(1)}, f32[32]{0:T(128)}, u32[]{:S(2)}) copy-start(f32[32]{0:T(128)} %get-tuple-element.27) | copy-start | bytes 388
  106.4 8.0 %copy-start.21 = (f32[32]{0:T(128)S(1)}, f32[32]{0:T(128)}, u32[]{:S(2)}) copy-start(f32[32]{0:T(128)} %get-tuple-element.28) | copy-start | bytes 388
  106.4 8.0 %copy-start.23 = (f32[32]{0:T(128)S(1)}, f32[32]{0:T(128)}, u32[]{:S(2)}) copy-start(f32[32]{0:T(128)} %get-tuple-element.29) | copy-start | bytes 388
  106.4 8.0 %copy-start.25 = (f32[32]{0:T(128)S(1)}, f32[32]{0:T(128)}, u32[]{:S(2)}) copy-start(f32[32]{0:T(128)} %get-tuple-element.30) | copy-start | bytes 388
  106.4 7.2 %collective-permute-start.7 = (f32[4,128,128]{2,1,0:T(8,128)S(1)}, f32[4,128,128]{2,1,0:T(8,128)S(1)}, u32[]{:S(2)}, u32[]{:S(2)}) collective-permute-start(f32[4,128,128]{2,1,0:T(8,128)S(1)} %get-tuple-element.15), channel_id=1, source_target_pairs={{1,0},{2,1},{3,2},{4,3},{5,4},{6,5},{7,6},{8,7},{9,8},{10,9},{11,1... | collective-permute-start | bytes 786440 | tf_op jit(solution)/shard_map/ppermute | solution.py:17
  114.4 18.1 %copy-start.6 = (bf16[128,128]{1,0:T(8,128)(2,1)S(1)}, bf16[128,128]{1,0:T(8,128)(2,1)}, u32[]{:S(2)}) copy-start(bf16[128,128]{1,0:T(8,128)(2,1)} %param.20) | copy-start | bytes 98308
  149.1 42.7 %all-to-all-start.2 = ((f32[128,1,1,2,16,128]{5,4,3,2,1,0:T(8,128)}), f32[128,1,1,2,16,128]{5,4,3,2,1,0:T(8,128)S(1)}, u32[]{:S(2)}, u32[]{:S(2)}) async-start(f32[128,1,1,2,16,128]{5,4,3,2,1,0:T(8,128)} %bitcast.52), calls=%async_computation.2 | async-start | bytes 4194304 | tf_op jit(solution)/shard_map/all_to_all | solution.py:40
  (8 other events, 17.9 us)
where the time goes:
time: 199 us; the launch traced here: 198 us
  matrix products  56.1 us (28%)
  waiting for transfers between devices  44.4 us (22%)
  starting transfers between devices  39.7 us (20%)
  local copies, waits for them, and re-layouts  33.3 us (17%)
  blocking collectives  20.9 us (11%)
    all_to_all x2, waiting for transfers between devices, one_exchange(): tiles = lax.all_to_all(tiles, axis, split_axis=0, concat_axis=0, tiled=True)  33.1 us
    dot_general x4, matrix products, stencil_sum(): jnp.einsum('xyw,zw->xyz', wavefield, stiff_z, precision=HIGH)  32.9 us
    all_to_all x1, blocking collectives, one_exchange(): tiles = lax.all_to_all(tiles, axis, split_axis=0, concat_axis=0, tiled=True)  20.9 us
    all_to_all x2, starting transfers between devices, one_exchange(): tiles = lax.all_to_all(tiles, axis, split_axis=0, concat_axis=0, tiled=True)  17.5 us
    dot_general x4, matrix products, stencil_sum(): result = jnp.einsum('yw,xwz->xyz', stiff_y, wavefield, precision=HIGH)  17.3 us
    ppermute x4, starting transfers between devices, padded_2(): before = lax.ppermute(last, axis, up)  16.5 us
    scatter x1, local copies, waits for them, and re-layouts, shards(): jnp.zeros((devices * capacity, rows_y, rows_z), jnp.float32).at[slot_ids]  13.6 us
    ppermute x4, waiting for transfers between devices, padded_2(): after = lax.ppermute(initial, axis, down)  10.1 us
  transfers between devices with their start and end apart: 10, of which 6 were waited for; matrix products, arithmetic and copies ran while one was open for 11% of the time, Pallas kernels for 0%

commit v1 on v0

v1 whole, which is shorter than its diff:
```python
import functools

import jax
import jax.numpy as jnp
from jax import lax
from jax.experimental import pallas as pl
from jax.experimental.pallas import tpu as pltpu
from jax.sharding import PartitionSpec as P

F32 = jnp.float32
BF16 = jnp.bfloat16
I32 = jnp.int32
MESH = pl.DeviceIdType.MESH
ROWS = 8
LANES = 128


def split(value):
    high = value.astype(BF16)
    low = (value - high.astype(F32)).astype(BF16)
    return high, low


def iota(shape, dim):
    return lax.broadcasted_iota(I32, shape, dim)


def dot(a, b):
    return jnp.dot(a, b, preferred_element_type=F32)


def window_kernel(
    cfg,
    prev_hbm,
    now_hbm,
    adj_hbm,
    back_hbm,
    coeffs,
    live,
    stiff_y,
    stiff_z,
    interp_y,
    interp_z,
    model,
    ids_in,
    wave_out,
    grad_out,
    u_a,
    u_b,
    u_hl,
    speed,
    kern,
    adj,
    ku0,
    halo,
    w_y,
    w_z,
    w_fwd,
    w_bwd,
    w_iz,
    id_one,
    id_two,
    id_all,
    idx_own,
    idx_req,
    own_sm,
    req_sm,
    f_a,
    f_b,
    f_ra,
    f_rb,
    f_in,
    tiles,
    g_tiles,
    g_a,
    g_b,
    g_ra,
    g_rb,
    g_in,
    one_hot,
    load_sem,
    idx_sem,
    id1_send,
    id1_recv,
    id2_send,
    id2_recv,
    h_send,
    h_recv,
    fa1_send,
    fa1_recv,
    fa2_send,
    fa2_recv,
    fb1_send,
    fb1_recv,
    fb2_send,
    fb2_recv,
    f_loc,
    ga1_send,
    ga1_recv,
    ga2_send,
    ga2_recv,
    gb1_send,
    gb1_recv,
    gb2_send,
    gb2_recv,
    g_loc,
    out_sem,
):
    ne, ns, planes, reach, steps, n_tiles, rows_t, blk, rows_b = cfg
    nb = ne * ns
    e = lax.axis_index("event")
    s = lax.axis_index("slab")
    own_dev = e * ns + s

    load_now = pltpu.make_async_copy(now_hbm.at[0], u_a.at[pl.ds(reach, planes)], load_sem.at[0])
    load_prev = pltpu.make_async_copy(prev_hbm.at[0], u_b.at[pl.ds(reach, planes)], load_sem.at[1])
    load_back = pltpu.make_async_copy(back_hbm.at[0], speed, load_sem.at[2])
    load_adj = [
        pltpu.make_async_copy(adj_hbm.at[0, i], adj.at[i], load_sem.at[3 + i]) for i in range(steps)
    ]
    load_now.start()
    load_prev.start()
    load_back.start()

    barrier = pltpu.get_barrier_semaphore()
    for d in range(1, ne):
        pl.semaphore_signal(
            barrier, inc=1, device_id=(lax.rem(e + d, ne), s), device_id_type=MESH
        )
    for d in range(1, ns):
        pl.semaphore_signal(
            barrier, inc=1, device_id=(e, lax.rem(s + d, ns)), device_id_type=MESH
        )
    pl.semaphore_wait(barrier, ne - 1 + ns - 1)

    def event_copy(src, dst, send, recv, d):
        return pltpu.make_async_remote_copy(
            src_ref=src,
            dst_ref=dst,
            send_sem=send.at[d],
            recv_sem=recv.at[d],
            device_id=(lax.rem(e + d, ne), s),
            device_id_type=MESH,
        )

    def slab_copy(src, dst, send, recv, d):
        return pltpu.make_async_remote_copy(
            src_ref=src,
            dst_ref=dst,
            send_sem=send.at[d],
            recv_sem=recv.at[d],
            device_id=(e, lax.rem(s + d, ns)),
            device_id_type=MESH,
        )

    ids = jnp.broadcast_to(ids_in[...], (ROWS, LANES))
    id_one[e] = ids
    hop1 = [event_copy(id_one.at[e], id_one.at[e], id1_send, id1_recv, d) for d in range(1, ne)]
    for c in hop1:
        c.start()
    for c in load_adj:
        c.start()

    ids_full = jnp.broadcast_to(ids_in[...], (LANES, LANES))
    owners = lax.shift_right_arithmetic(ids_full, cfg_shift(blk))
    owners_t = jnp.transpose(owners)
    row_i = iota((LANES, LANES), 0)
    lane_i = iota((LANES, LANES), 1)
    earlier = jnp.where((owners == owners_t) & (row_i < lane_i), 1, 0)
    rank = jnp.sum(earlier, axis=0, keepdims=True)
    owner_row = owners[0:1]
    at_e = owner_row // ns
    at_s = owner_row - at_e * ns
    live_n = live[0, 0]
    lane_row = iota((1, LANES), 1)
    address = jnp.where(rank == 0, at_s * ne + at_e, nb + owner_row)
    address = jnp.where(lane_row < live_n, address, 2 * nb)
    none = LANES
    match = owners == row_i
    first = jnp.min(jnp.where(match, lane_i, none), axis=1, keepdims=True)
    second = jnp.min(jnp.where(match & (lane_i > first), lane_i, none), axis=1, keepdims=True)

    def as_row(column):
        return jnp.transpose(jnp.broadcast_to(column, (LANES, LANES)))[0:1]

    tile_0 = as_row(first)
    tile_1 = as_row(second)
    tile_0 = jnp.where(tile_0 < live_n, tile_0, n_tiles)
    tile_1 = jnp.where(tile_1 < live_n, tile_1, n_tiles)
    sub = iota((ROWS, LANES), 0)
    table = jnp.where(
        sub == 0,
        jnp.broadcast_to(address, (ROWS, LANES)),
        jnp.where(
            sub == 1,
            jnp.broadcast_to(tile_0, (ROWS, LANES)),
            jnp.broadcast_to(tile_1, (ROWS, LANES)),
        ),
    )
    idx_own[...] = table
    own_copy = pltpu.make_async_copy(idx_own, own_sm, idx_sem.at[0])
    own_copy.start()

    high, low = split(stiff_y[...])
    w_y[...] = jnp.concatenate(
        [jnp.concatenate([high, high], axis=1), jnp.concatenate([low, low], axis=1)], axis=0
    )
    high, low = split(jnp.transpose(stiff_z[...]))
    half = jnp.concatenate([high, low], axis=1)
    w_z[...] = jnp.concatenate([half, half], axis=0)

    for c in hop1:
        c.wait()
    gathered = jnp.full((ROWS, LANES), -1, I32)
    for i in range(ne):
        gathered = jnp.where(sub == i, id_one[i], gathered)
    id_two[...] = gathered
    for i in range(LANES // ROWS):
        if i >= ns:
            id_all[i] = jnp.full((ROWS, LANES), -1, I32)
    id_all[s] = gathered
    hop2 = [slab_copy(id_two, id_all.at[s], id2_send, id2_recv, d) for d in range(1, ns)]
    for c in hop2:
        c.start()

    load_now.wait()
    zero_halo = jnp.zeros((reach,) + u_a.shape[1:], F32)
    for buf in (u_a, u_b):
        buf[pl.ds(0, reach)] = zero_halo
        buf[pl.ds(reach + planes, reach)] = zero_halo

    def split_planes(i, carry):
        high, low = split(u_a[reach + i])
        u_hl[i, 0] = high
        u_hl[i, 1] = low
        return carry

    lax.fori_loop(0, planes, split_planes, 0)

    def halo_copy(step, side):
        start = 0 if side == 0 else planes - reach
        return pltpu.make_async_remote_copy(
            src_ref=u_hl.at[pl.ds(start, reach), 0],
            dst_ref=halo.at[step, side],
            send_sem=h_send.at[step, side],
            recv_sem=h_recv.at[step, side],
            device_id=(e, lax.rem(s + (ns - 1 if side == 0 else 1), ns)),
            device_id_type=MESH,
        )

    def send_halos(step):
        @pl.when(s > 0)
        def _():
            halo_copy(step, 0).start()

        @pl.when(s < ns - 1)
        def _():
            halo_copy(step, 1).start()

    def take_halos(step, buf):
        @pl.when(s > 0)
        def _():
            halo_copy(step, 0).wait_send()
            halo_copy(step, 1).wait_recv()
            buf[pl.ds(0, reach)] = halo[step, 1].astype(F32)

        @pl.when(s < ns - 1)
        def _():
            halo_copy(step, 1).wait_send()
            halo_copy(step, 0).wait_recv()
            buf[pl.ds(reach + planes, reach)] = halo[step, 0].astype(F32)

    send_halos(0)

    for c in hop2:
        c.wait()
    asked_all = id_all[...].reshape(LANES, LANES)
    mine = lax.shift_right_arithmetic(asked_all, cfg_shift(blk)) == own_dev
    code = lane_i * blk + (asked_all & (blk - 1))
    none = LANES * blk
    code_0 = jnp.min(jnp.where(mine, code, none), axis=1, keepdims=True)
    code_1 = jnp.min(jnp.where(mine & (code > code_0), code, none), axis=1, keepdims=True)
    asked_0 = as_row(code_0) & (blk - 1)
    asked_1 = as_row(code_1) & (blk - 1)
    idx_req[...] = jnp.where(
        sub == 0,
        jnp.broadcast_to(asked_0, (ROWS, LANES)),
        jnp.broadcast_to(asked_1, (ROWS, LANES)),
    )
    req_copy = pltpu.make_async_copy(idx_req, req_sm, idx_sem.at[1])
    req_copy.start()
    req_copy.wait()

    def find_blocks(i, carry):
        for j in range(ne):
            f_a[j, i] = model[req_sm[0, i * ROWS + j]]
            f_b[i, j] = model[req_sm[1, i * ROWS + j]]
        return carry

    lax.fori_loop(0, ns, find_blocks, 0)

    def exchange(a, b, ra, rb, out, sems, loc):
        a1s, a1r, a2s, a2r, b1s, b1r, b2s, b2r = sems
        a1 = [
            event_copy(a.at[lax.rem(e + d, ne)], ra.at[e], a1s, a1r, d) for d in range(1, ne)
        ]
        b1 = [slab_copy(b.at[lax.rem(s + d, ns)], rb.at[s], b1s, b1r, d) for d in range(1, ns)]
        here = [
            pltpu.make_async_copy(a.at[e], ra.at[e], loc.at[0]),
            pltpu.make_async_copy(b.at[s], rb.at[s], loc.at[1]),
        ]
        a2 = [
            slab_copy(
                ra.at[:, lax.rem(s + d, ns)], out.at[pl.ds(s * ne, ne)], a2s, a2r, d
            )
            for d in range(1, ns)
        ]
        b2 = [
            event_copy(
                rb.at[:, lax.rem(e + d, ne)], out.at[pl.ds(nb + e * ns, ns)], b2s, b2r, d
            )
            for d in range(1, ne)
        ]
        there = [
            pltpu.make_async_copy(ra.at[:, s], out.at[pl.ds(s * ne, ne)], loc.at[2]),
            pltpu.make_async_copy(rb.at[:, e], out.at[pl.ds(nb + e * ns, ns)], loc.at[3]),
        ]

        def begin():
            for c in a1 + b1 + here:
                c.start()

        def middle():
            for c in here[:1] + a1:
                c.wait()
            for c in a2 + there[:1]:
                c.start()
            for c in here[1:] + b1:
                c.wait()
            for c in b2 + there[1:]:
                c.start()

        def end():
            for c in a2 + b2 + there:
                c.wait()

        return begin, middle, end

    begin, middle, end = exchange(
        f_a,
        f_b,
        f_ra,
        f_rb,
        f_in,
        (fa1_send, fa1_recv, fa2_send, fa2_recv, fb1_send, fb1_recv, fb2_send, fb2_recv),
        f_loc,
    )
    begin()

    tiles_y = LANES // rows_t
    half_rows = tiles_y * rows_b
    pick_b = jnp.where(iota((half_rows, rows_b), 0) % rows_b == iota((half_rows, rows_b), 1), 1.0, 0.0)
    pick_y = jnp.where(iota((rows_t, LANES), 1) % rows_t == iota((rows_t, LANES), 0), 1.0, 0.0)
    wide = dot(pick_b.astype(BF16), interp_y[...]).astype(BF16)
    wide = dot(wide, pick_y.astype(BF16))
    on_diag = iota((half_rows, LANES), 0) // rows_b == iota((half_rows, LANES), 1) // rows_t
    diag = jnp.where(on_diag, wide, 0.0)
    w_bwd[...] = diag.astype(BF16)
    w_fwd[...] = jnp.transpose(jnp.concatenate([diag, diag], axis=0)).astype(BF16)
    iz_t = jnp.transpose(interp_z[...].astype(F32)).astype(BF16)
    w_iz[...] = jnp.concatenate([iz_t, iz_t], axis=0)

    ny = LANES

    def stiff_pair(x):
        a, b = u_hl[x, 0], u_hl[x, 1]
        c, d = u_hl[x + 1, 0], u_hl[x + 1, 1]
        left = jnp.concatenate(
            [jnp.concatenate([a, b], axis=1), jnp.concatenate([c, d], axis=1)], axis=0
        )
        right = jnp.concatenate(
            [jnp.concatenate([a, c], axis=1), jnp.concatenate([b, d], axis=1)], axis=0
        )
        along_z = dot(left, w_z[...])
        along_z = along_z[:, :LANES] + along_z[:, LANES:]
        along_y = dot(w_y[...], right)
        along_y = along_y[:ny] + along_y[ny:]
        return along_z[:ny] + along_y[:, :LANES], along_z[ny:] + along_y[:, LANES:]

    def stencil(buf, x):
        total = coeffs[0, x, 0] * buf[x]
        for k in range(1, 2 * reach + 1):
            total = total + coeffs[0, x, k] * buf[x + k]
        return total

    pairs = planes // 2
    edge = reach // 2

    def over_planes(body, before_edges):
        def interior(i, carry):
            body(2 * i)
            return carry

        lax.fori_loop(edge, pairs - edge, interior, 0)
        before_edges()

        def edges(i, carry):
            body(2 * jnp.where(i < edge, i, pairs - 2 * edge + i))
            return carry

        lax.fori_loop(0, 2 * edge, edges, 0)

    def first_stiff(x):
        for p, part in enumerate(stiff_pair(x)):
            ku0[x + p] = part + stencil(u_a, x + p)

    over_planes(first_stiff, lambda: take_halos(0, u_a))
    middle()
    f_in[2 * nb] = jnp.zeros(f_in.shape[1:], BF16)

    ids_f = jnp.where(
        sub == 0,
        jnp.broadcast_to(asked_0, (ROWS, LANES)),
        jnp.broadcast_to(asked_1, (ROWS, LANES)),
    ).astype(F32).astype(BF16)

    slots = ns * ne

    def spread(rank_row, position, base):
        width = slots * rows_b
        chunk = min(512, width)
        for c0 in range(0, width, chunk):
            lane = iota((LANES, chunk), 1) + c0
            source = position(lane // rows_b)
            pick = jnp.where(iota((LANES, chunk), 0) == source, 1.0, 0.0).astype(BF16)
            key = dot(ids_f, pick)[rank_row : rank_row + 1].astype(I32) * rows_b
            key = key + (iota((1, chunk), 1) + c0) % rows_b
            rows = blk * rows_b
            hot = jnp.where(
                jnp.broadcast_to(key, (rows, chunk)) == iota((rows, chunk), 0), 1.0, 0.0
            )
            one_hot[:, base + c0 : base + c0 + chunk] = hot.astype(BF16)

    spread(0, lambda slot: (slot // ne) * ROWS + slot % ne, 0)
    spread(1, lambda slot: (slot % ns) * ROWS + slot // ns, slots * rows_b)

    own_copy.wait()
    load_back.wait()
    load_prev.wait()
    end()

    def take_tile(i, carry):
        tiles[i] = f_in[own_sm[0, i]]
        return carry

    lax.fori_loop(0, n_tiles, take_tile, 0, unroll=8)

    def speed_pair(i, carry):
        x = 2 * i
        blocks = tiles[pl.ds(x * tiles_y, 2 * tiles_y)].reshape(2 * half_rows, LANES)
        high, low = split(dot(blocks, interp_z[...]))
        right = jnp.concatenate(
            [
                jnp.concatenate([high[:half_rows], high[half_rows:]], axis=1),
                jnp.concatenate([low[:half_rows], low[half_rows:]], axis=1),
            ],
            axis=0,
        )
        perturb = dot(w_fwd[...], right)
        speed[x] = speed[x] * jnp.exp(perturb[:, :LANES])
        speed[x + 1] = speed[x + 1] * jnp.exp(perturb[:, LANES:])
        return carry

    lax.fori_loop(0, pairs, speed_pair, 0)

    def advance(x, force, step, now, prev):
        change = speed[x] * force
        drawn = adj[step, x] * change
        if step == 0:
            kern[x] = -drawn
        elif step < steps - 1:
            kern[x] = kern[x] - drawn
        else:
            total = (kern[x] - drawn).astype(BF16)
            u_hl[x, 1] = total
        later = 2.0 * now[x + reach] - prev[x + reach] - change
        prev[x + reach] = later
        if step < steps - 1:
            high, low = split(later)
            u_hl[x, 0] = high
            u_hl[x, 1] = low

    load_adj[0].wait()

    def first_step(i, carry):
        advance(i, ku0[i], 0, u_a, u_b)
        return carry

    lax.fori_loop(0, planes, first_step, 0)
    if steps > 1:
        send_halos(1)
    now, prev = u_b, u_a
    for step in range(1, steps):
        load_adj[step].wait()

        def body(x):
            parts = stiff_pair(x)
            for p in range(2):
                advance(x + p, parts[p] + stencil(now, x + p), step, now, prev)

        over_planes(body, functools.partial(take_halos, step, now))
        if step < steps - 1:
            send_halos(step + 1)
        now, prev = prev, now

    wave_copy = pltpu.make_async_copy(now.at[pl.ds(reach, planes)], wave_out.at[0], out_sem)
    wave_copy.start()

    def grad_pair(i, carry):
        x = 2 * i
        right = jnp.concatenate([u_hl[x, 1], u_hl[x + 1, 1]], axis=1)
        back = dot(w_bwd[...], right)
        parts = []
        for p in range(2):
            high, low = split(back[:, p * LANES : (p + 1) * LANES])
            parts.append(jnp.concatenate([high, low], axis=1))
        grads = dot(jnp.concatenate(parts, axis=0), w_iz[...])
        g_tiles[pl.ds(x * tiles_y, 2 * tiles_y)] = grads.astype(BF16).reshape(
            2 * tiles_y, rows_b, LANES
        )
        return carry

    lax.fori_loop(0, pairs, grad_pair, 0)
    g_tiles[n_tiles] = jnp.zeros(g_tiles.shape[1:], BF16)

    def pack(i, carry):
        for j in range(ne):
            g_a[j, i] = g_tiles[own_sm[1, j * ns + i]]
            g_b[i, j] = g_tiles[own_sm[2, j * ns + i]]
        return carry

    lax.fori_loop(0, ns, pack, 0)
    begin, middle, end = exchange(
        g_a,
        g_b,
        g_ra,
        g_rb,
        g_in,
        (ga1_send, ga1_recv, ga2_send, ga2_recv, gb1_send, gb1_recv, gb2_send, gb2_recv),
        g_loc,
    )
    begin()
    middle()
    end()
    received = g_in[...].reshape(2 * nb * rows_b, LANES)
    total = dot(one_hot[...], received)
    grad_out[...] = total.reshape(grad_out.shape)
    wave_copy.wait()


def cfg_shift(blk):
    return blk.bit_length() - 1


def shards(
    wave_prev,
    wave_now,
    adjoint,
    background,
    coeffs_x,
    stiff_y,
    stiff_z,
    interp_y,
    interp_z,
    model,
    block_index,
    live_count,
):
    ne = lax.axis_size("event")
    ns = lax.axis_size("slab")
    nb = ne * ns
    blk, rows_b, _ = model.shape
    planes, ny, nz = wave_now.shape[1:]
    steps = adjoint.shape[1]
    reach = (coeffs_x.shape[2] - 1) // 2
    tiles_y = block_index.shape[2]
    n_tiles = planes * tiles_y
    rows_t = ny // tiles_y
    ids = block_index.reshape(1, n_tiles)
    if n_tiles < LANES:
        ids = jnp.pad(ids, ((0, 0), (0, LANES - n_tiles)), constant_values=-1)
    cfg = (ne, ns, planes, reach, steps, n_tiles, rows_t, blk, rows_b)
    dma = pltpu.SemaphoreType.DMA
    vmem = pltpu.VMEM
    slot = (rows_b, nz)

    def buffers():
        return [
            vmem((ne, ns) + slot, BF16),
            vmem((ns, ne) + slot, BF16),
            vmem((ne, ns) + slot, BF16),
            vmem((ns, ne) + slot, BF16),
        ]

    def sems():
        return [dma((n,)) for n in (ne, ne, ns, ns, ns, ns, ne, ne)] + [dma((4,))]

    fetch = buffers()
    grads = buffers()
    whole = pl.BlockSpec(memory_space=pltpu.VMEM)
    smem = pl.BlockSpec(memory_space=pltpu.SMEM)
    hbm = pl.BlockSpec(memory_space=pl.ANY)
    wave, grad = pl.pallas_call(
        functools.partial(window_kernel, cfg),
        out_shape=(
            jax.ShapeDtypeStruct(wave_now.shape, F32),
            jax.ShapeDtypeStruct(model.shape, F32),
        ),
        in_specs=[hbm] * 4 + [smem] * 2 + [whole] * 6,
        out_specs=(hbm, whole),
        scratch_shapes=[
            vmem((planes + 2 * reach, ny, nz), F32),
            vmem((planes + 2 * reach, ny, nz), F32),
            vmem((planes, 2, ny, nz), BF16),
            vmem((planes, ny, nz), F32),
            vmem((planes, ny, nz), F32),
            vmem((steps, planes, ny, nz), F32),
            vmem((planes, ny, nz), F32),
            vmem((steps, 2, reach, ny, nz), BF16),
            vmem((2 * ny, 2 * ny), BF16),
            vmem((2 * nz, 2 * nz), BF16),
            vmem((ny, 2 * tiles_y * rows_b), BF16),
            vmem((tiles_y * rows_b, ny), BF16),
            vmem((2 * nz, nz), BF16),
            vmem((ne, ROWS, LANES), I32),
            vmem((ROWS, LANES), I32),
            vmem((LANES // ROWS, ROWS, LANES), I32),
            vmem((ROWS, LANES), I32),
            vmem((ROWS, LANES), I32),
            pltpu.SMEM((ROWS, LANES), I32),
            pltpu.SMEM((ROWS, LANES), I32),
            *fetch,
            vmem((2 * nb + 1,) + slot, BF16),
            vmem((n_tiles,) + slot, BF16),
            vmem((n_tiles + 1,) + slot, BF16),
            *grads,
            vmem((2 * nb,) + slot, BF16),
            vmem((blk * rows_b, 2 * nb * rows_b), BF16),
            dma((3 + steps,)),
            dma((2,)),
            dma((ne,)),
            dma((ne,)),
            dma((ns,)),
            dma((ns,)),
            dma((steps, 2)),
            dma((steps, 2)),
            *sems(),
            *sems(),
            dma,
        ],
        compiler_params=pltpu.CompilerParams(
            collective_id=0, has_side_effects=True, vmem_limit_bytes=56 * 1024 * 1024
        ),
        name="window",
    )(
        wave_prev,
        wave_now,
        adjoint,
        background,
        coeffs_x,
        live_count,
        stiff_y,
        stiff_z,
        interp_y,
        interp_z,
        model,
        ids,
    )
    return wave, grad


def solution(mesh):
    return jax.shard_map(
        shards,
        mesh=mesh,
        in_specs=(
            P("event", "slab", None, None),
            P("event", "slab", None, None),
            P("event", None, "slab", None, None),
            P("event", "slab", None, None),
            P("event", "slab", None),
            P(),
            P(),
            P(),
            P(),
            P(("event", "slab"), None, None),
            P("event", "slab", None),
            P("event", "slab"),
        ),
        out_specs=(P("event", "slab", None, None), P(("event", "slab"), None, None)),
        check_vma=False,
    )
```

time: 199 us -> 92.9 us (0.47)
  Pallas kernels: 0 us -> 84.7 us
  matrix products: 56.1 us -> 0 us
  waiting for transfers between devices: 44.4 us -> 0 us
  starting transfers between devices: 39.7 us -> 0 us
  local copies, waits for them, and re-layouts: 33.3 us -> 6.58 us
  blocking collectives: 20.9 us -> 0 us
    pallas_call x0 -> x1, Pallas kernels: none -> 84.7 us  [shards(): pl.pallas_call(functools.partial(window_kernel, cfg), out_shape=(jax.Shap...]
    dot_general x13 -> x0, matrix products: 56.1 us -> none  [the longest x4 32.9 us: stencil_sum(): jnp.einsum('xyw,zw->xyz', wavefield, stiff_z, precision=HIGH)]
    all_to_all x2 -> x0, waiting for transfers between devices: 33.1 us -> none  [one_exchange(): tiles = lax.all_to_all(tiles, axis, split_axis=0, concat_axis=0, tiled=True)]
    ppermute x8 -> x0, starting transfers between devices: 22.2 us -> none  [the longest x4 16.5 us: padded_2(): before = lax.ppermute(last, axis, up)]
    all_to_all x1 -> x0, blocking collectives: 20.9 us -> none  [one_exchange(): tiles = lax.all_to_all(tiles, axis, split_axis=0, concat_axis=0, tiled=True)]
    all_to_all x2 -> x0, starting transfers between devices: 17.5 us -> none  [one_exchange(): tiles = lax.all_to_all(tiles, axis, split_axis=0, concat_axis=0, tiled=True)]
    scatter x2 -> x0, local copies, waits for them, and re-layouts: 14.6 us -> none  [the longest x1 13.6 us: shards(): jnp.zeros((devices * capacity, rows_y, rows_z), jnp.float32).at[slot_ids]]
    ppermute x8 -> x0, waiting for transfers between devices: 11.2 us -> none  [the longest x4 10.1 us: padded_2(): after = lax.ppermute(initial, axis, down)]
  transfers between devices with their start and end apart: 10 -> 0, of which waited for: 6 -> 0; matrix products, arithmetic and copies ran while one was open for 11% -> 0% of each run, Pallas kernels for 0% -> 0%
where the time goes in v1:
time: 92.9 us; the launch traced here: 92.6 us
  Pallas kernels  84.7 us (91%)
  local copies, waits for them, and re-layouts  6.58 us (7%)
  between operations  1.3 us (1%)
    pallas_call x1, Pallas kernels, shards(): pl.pallas_call(functools.partial(window_kernel, cfg), out_shape=(jax.Shap...  84.7 us
    unnamed x6, local copies, waits for them, and re-layouts  5.96 us

profile of v1, /device:TPU:1, one launch (start us, length us, event | category | flops | bytes accessed | tf_op | source)
XLA Modules:
  0.0 92.6 jit_solution(7617515761860073688)
XLA Ops:
  1.3 1.4 %copy.17.coeffs = f32[1,32,9]{2,1,0:T(8,128)} copy(f32[1,32,9]{1,0,2:T(1,128)} %param.16) | data formatting | bytes 2304 | tf_op args[4]
  2.6 0.8 copy.16
  3.4 0.6 reshape.7.ids_in
  4.0 84.7 %window.1 = (f32[1,32,128,128]{3,2,1,0:T(8,128)}, f32[16,16,128]{2,1,0:T(8,128)}) custom-call(f32[1,32,128,128]{3,2,1,0:T(8,128)} %prev_hbm.1, f32[1,32,128,128]{3,2,1,0:T(8,128)} %now_hbm.1, f32[1,4,32,128,128]{4,3,2,1,0:T(8,128)} %adj_hbm.1, f32[1,32,128,128]{3,2,1,0:T(8,128)} %back_hbm.1, f32[1,32,9]{2,1,0:T(8,128)} %copy.17.coeffs, ...), custom_call_target="tpu_custom_call" | custom-call | tf_op jit(solution)/shard_map/window/pallas_call | solution.py:613
  88.8 0.0 copy-start
  88.8 3.2 %copy.21 = f32[1,32,128,128]{3,2,1,0:T(8,128)} copy(f32[1,32,128,128]{3,2,1,0:T(8,128)} %get-tuple-element.4) | data formatting | bytes 4194304
  92.0 0.0 copy-done
  92.0 0.7 copy.22
Async XLA Ops:
  88.8 3.2 %copy-start = (f32[16,16,128]{2,1,0:T(8,128)S(1)}, f32[16,16,128]{2,1,0:T(8,128)}, u32[]{:S(2)}) copy-start(f32[16,16,128]{2,1,0:T(8,128)} %get-tuple-element.5) | copy-start | bytes 393220

commit v2 on v1

--- a/solution.py
+++ b/solution.py
@@ -35,7 +35,7 @@
     now_hbm,
     adj_hbm,
     back_hbm,
-    coeffs,
+    coeffs_hbm,
     live,
     stiff_y,
     stiff_z,
@@ -58,17 +58,16 @@
     w_fwd,
     w_bwd,
     w_iz,
-    id_one,
-    id_two,
+    coeffs,
+    id_own,
     id_all,
     idx_own,
     idx_req,
+    asked_all,
     own_sm,
     req_sm,
-    f_a,
-    f_b,
-    f_ra,
-    f_rb,
+    column,
+    f_out,
     f_in,
     tiles,
     g_tiles,
@@ -80,20 +79,16 @@
     one_hot,
     load_sem,
     idx_sem,
-    id1_send,
-    id1_recv,
-    id2_send,
-    id2_recv,
+    id_send,
+    id_recv,
+    col_send,
+    col_recv,
+    ask_send,
+    ask_recv,
+    f_send,
+    f_recv,
     h_send,
     h_recv,
-    fa1_send,
-    fa1_recv,
-    fa2_send,
-    fa2_recv,
-    fb1_send,
-    fb1_recv,
-    fb2_send,
-    fb2_recv,
     f_loc,
     ga1_send,
     ga1_recv,
@@ -110,7 +105,7 @@
     nb = ne * ns
     e = lax.axis_index("event")
     s = lax.axis_index("slab")
-    own_dev = e * ns + s
+    tiles_y = LANES // rows_t
 
     load_now = pltpu.make_async_copy(now_hbm.at[0], u_a.at[pl.ds(reach, planes)], load_sem.at[0])
     load_prev = pltpu.make_async_copy(prev_hbm.at[0], u_b.at[pl.ds(reach, planes)], load_sem.at[1])
@@ -118,7 +113,9 @@
     load_adj = [
         pltpu.make_async_copy(adj_hbm.at[0, i], adj.at[i], load_sem.at[3 + i]) for i in range(steps)
     ]
+    load_coeffs = pltpu.make_async_copy(coeffs_hbm, coeffs, idx_sem.at[2])
     load_now.start()
+    load_coeffs.start()
     load_prev.start()
     load_back.start()
 
@@ -153,16 +150,28 @@
             device_id_type=MESH,
         )
 
-    ids = jnp.broadcast_to(ids_in[...], (ROWS, LANES))
-    id_one[e] = ids
-    hop1 = [event_copy(id_one.at[e], id_one.at[e], id1_send, id1_recv, d) for d in range(1, ne)]
-    for c in hop1:
+    column_copies = [event_copy(model, column.at[e], col_send, col_recv, d) for d in range(1, ne)]
+    sub = iota((ROWS, LANES), 0)
+    planes_id = ids_in[0]
+    ids_row = jnp.concatenate([planes_id[q : q + 1] for q in range(tiles_y)], axis=1)
+    if n_tiles < LANES:
+        ids_row = jnp.concatenate([ids_row, jnp.full((1, LANES - n_tiles), -1, I32)], axis=1)
+    ids = jnp.broadcast_to(ids_row, (ROWS, LANES))
+    id_own[...] = ids
+    for i in range(LANES // ROWS):
+        if i >= ns:
+            id_all[i] = jnp.full((ROWS, LANES), -1, I32)
+    id_all[s] = ids
+    id_copies = [slab_copy(id_own, id_all.at[s], id_send, id_recv, d) for d in range(1, ns)]
+    for c in id_copies:
         c.start()
+    for c in column_copies:
+        c.start()
+    column[e] = model[...]
     for c in load_adj:
         c.start()
 
-    ids_full = jnp.broadcast_to(ids_in[...], (LANES, LANES))
-    owners = lax.shift_right_arithmetic(ids_full, cfg_shift(blk))
+    owners = lax.shift_right_arithmetic(jnp.broadcast_to(ids_row, (LANES, LANES)), cfg_shift(blk))
     owners_t = jnp.transpose(owners)
     row_i = iota((LANES, LANES), 0)
     lane_i = iota((LANES, LANES), 1)
@@ -172,23 +181,28 @@
     at_e = owner_row // ns
     at_s = owner_row - at_e * ns
     live_n = live[0, 0]
-    lane_row = iota((1, LANES), 1)
-    address = jnp.where(rank == 0, at_s * ne + at_e, nb + owner_row)
-    address = jnp.where(lane_row < live_n, address, 2 * nb)
+
+    def in_order(lane):
+        return lane % planes * tiles_y + lane // planes
+
+    address = at_s * (2 * ne) + rank * ne + at_e
+    alive = in_order(iota((1, LANES), 1)) < live_n
+    address = jnp.where(alive, address, 2 * nb)
     none = LANES
     match = owners == row_i
     first = jnp.min(jnp.where(match, lane_i, none), axis=1, keepdims=True)
     second = jnp.min(jnp.where(match & (lane_i > first), lane_i, none), axis=1, keepdims=True)
 
-    def as_row(column):
-        return jnp.transpose(jnp.broadcast_to(column, (LANES, LANES)))[0:1]
-
-    tile_0 = as_row(first)
-    tile_1 = as_row(second)
-    tile_0 = jnp.where(tile_0 < live_n, tile_0, n_tiles)
-    tile_1 = jnp.where(tile_1 < live_n, tile_1, n_tiles)
-    sub = iota((ROWS, LANES), 0)
-    table = jnp.where(
+    def as_row(values):
+        return jnp.transpose(jnp.broadcast_to(values, (LANES, LANES)))[0:1]
+
+    def tile_at(lane):
+        tile = in_order(lane)
+        return jnp.where((lane < none) & (tile < live_n), tile, n_tiles)
+
+    tile_0 = tile_at(as_row(first))
+    tile_1 = tile_at(as_row(second))
+    idx_own[...] = jnp.where(
         sub == 0,
         jnp.broadcast_to(address, (ROWS, LANES)),
         jnp.where(
@@ -197,7 +211,6 @@
             jnp.broadcast_to(tile_1, (ROWS, LANES)),
         ),
     )
-    idx_own[...] = table
     own_copy = pltpu.make_async_copy(idx_own, own_sm, idx_sem.at[0])
     own_copy.start()
 
@@ -209,33 +222,13 @@
     half = jnp.concatenate([high, low], axis=1)
     w_z[...] = jnp.concatenate([half, half], axis=0)
 
-    for c in hop1:
-        c.wait()
-    gathered = jnp.full((ROWS, LANES), -1, I32)
-    for i in range(ne):
-        gathered = jnp.where(sub == i, id_one[i], gathered)
-    id_two[...] = gathered
-    for i in range(LANES // ROWS):
-        if i >= ns:
-            id_all[i] = jnp.full((ROWS, LANES), -1, I32)
-    id_all[s] = gathered
-    hop2 = [slab_copy(id_two, id_all.at[s], id2_send, id2_recv, d) for d in range(1, ns)]
-    for c in hop2:
-        c.start()
-
     load_now.wait()
-    zero_halo = jnp.zeros((reach,) + u_a.shape[1:], F32)
-    for buf in (u_a, u_b):
-        buf[pl.ds(0, reach)] = zero_halo
-        buf[pl.ds(reach + planes, reach)] = zero_halo
 
     def split_planes(i, carry):
         high, low = split(u_a[reach + i])
         u_hl[i, 0] = high
         u_hl[i, 1] = low
         return carry
-
-    lax.fori_loop(0, planes, split_planes, 0)
 
     def halo_copy(step, side):
         start = 0 if side == 0 else planes - reach
@@ -248,56 +241,70 @@
             device_id_type=MESH,
         )
 
-    def send_halos(step):
-        @pl.when(s > 0)
+    def send_halo(step, side):
+        @pl.when(s > 0 if side == 0 else s < ns - 1)
         def _():
-            halo_copy(step, 0).start()
-
-        @pl.when(s < ns - 1)
+            halo_copy(step, side).start()
+
+    def take_halo(step, side, buf):
+        @pl.when(s > 0 if side == 0 else s < ns - 1)
         def _():
-            halo_copy(step, 1).start()
-
-    def take_halos(step, buf):
-        @pl.when(s > 0)
-        def _():
-            halo_copy(step, 0).wait_send()
-            halo_copy(step, 1).wait_recv()
-            buf[pl.ds(0, reach)] = halo[step, 1].astype(F32)
-
-        @pl.when(s < ns - 1)
-        def _():
-            halo_copy(step, 1).wait_send()
-            halo_copy(step, 0).wait_recv()
-            buf[pl.ds(reach + planes, reach)] = halo[step, 0].astype(F32)
-
-    send_halos(0)
-
-    for c in hop2:
+            halo_copy(step, side).wait_send()
+            halo_copy(step, 1 - side).wait_recv()
+            at = 0 if side == 0 else reach + planes
+            buf[pl.ds(at, reach)] = halo[step, 1 - side].astype(F32)
+
+    lax.fori_loop(0, reach, split_planes, 0, unroll=2)
+    lax.fori_loop(planes - reach, planes, split_planes, 0, unroll=2)
+    send_halo(0, 0)
+    send_halo(0, 1)
+    lax.fori_loop(reach, planes - reach, split_planes, 0, unroll=2)
+    zero_halo = jnp.zeros((reach,) + u_a.shape[1:], F32)
+    for buf in (u_a, u_b):
+        buf[pl.ds(0, reach)] = zero_halo
+        buf[pl.ds(reach + planes, reach)] = zero_halo
+
+    for c in id_copies:
         c.wait()
-    asked_all = id_all[...].reshape(LANES, LANES)
-    mine = lax.shift_right_arithmetic(asked_all, cfg_shift(blk)) == own_dev
-    code = lane_i * blk + (asked_all & (blk - 1))
+    asked_ids = id_all[...].reshape(LANES, LANES)
+    wanted = (row_i % ROWS) * ns + s
+    mine = (lax.shift_right_arithmetic(asked_ids, cfg_shift(blk)) == wanted) & (row_i % ROWS < ne)
+    code = lane_i * blk + (asked_ids & (blk - 1))
     none = LANES * blk
     code_0 = jnp.min(jnp.where(mine, code, none), axis=1, keepdims=True)
     code_1 = jnp.min(jnp.where(mine & (code > code_0), code, none), axis=1, keepdims=True)
     asked_0 = as_row(code_0) & (blk - 1)
     asked_1 = as_row(code_1) & (blk - 1)
-    idx_req[...] = jnp.where(
+    asked = jnp.where(
         sub == 0,
         jnp.broadcast_to(asked_0, (ROWS, LANES)),
         jnp.broadcast_to(asked_1, (ROWS, LANES)),
     )
+    idx_req[...] = asked
     req_copy = pltpu.make_async_copy(idx_req, req_sm, idx_sem.at[1])
     req_copy.start()
+    asked_all[e] = asked
+    for c in column_copies:
+        c.wait()
     req_copy.wait()
-
-    def find_blocks(i, carry):
+    fetches = []
+    for d in [*range(1, ns), 0]:
+        to = lax.rem(s + d, ns)
         for j in range(ne):
-            f_a[j, i] = model[req_sm[0, i * ROWS + j]]
-            f_b[i, j] = model[req_sm[1, i * ROWS + j]]
-        return carry
-
-    lax.fori_loop(0, ns, find_blocks, 0)
+            f_out[to, j] = column[j, req_sm[0, to * ROWS + j]]
+            f_out[to, ne + j] = column[j, req_sm[1, to * ROWS + j]]
+        dst = f_in.at[pl.ds(s * (2 * ne), 2 * ne)]
+        if d == 0:
+            c = pltpu.make_async_copy(f_out.at[to], dst, f_loc)
+        else:
+            c = slab_copy(f_out.at[to], dst, f_send, f_recv, d)
+        c.start()
+        fetches.append(c)
+    ask_copies = [
+        event_copy(idx_req, asked_all.at[e], ask_send, ask_recv, d) for d in range(1, ne)
+    ]
+    for c in ask_copies:
+        c.start()
 
     def exchange(a, b, ra, rb, out, sems, loc):
         a1s, a1r, a2s, a2r, b1s, b1r, b2s, b2r = sems
@@ -310,20 +317,16 @@
             pltpu.make_async_copy(b.at[s], rb.at[s], loc.at[1]),
         ]
         a2 = [
-            slab_copy(
-                ra.at[:, lax.rem(s + d, ns)], out.at[pl.ds(s * ne, ne)], a2s, a2r, d
-            )
+            slab_copy(ra.at[:, lax.rem(s + d, ns)], out.at[0, :, s], a2s, a2r, d)
             for d in range(1, ns)
         ]
         b2 = [
-            event_copy(
-                rb.at[:, lax.rem(e + d, ne)], out.at[pl.ds(nb + e * ns, ns)], b2s, b2r, d
-            )
+            event_copy(rb.at[:, lax.rem(e + d, ne)], out.at[1, e], b2s, b2r, d)
             for d in range(1, ne)
         ]
         there = [
-            pltpu.make_async_copy(ra.at[:, s], out.at[pl.ds(s * ne, ne)], loc.at[2]),
-            pltpu.make_async_copy(rb.at[:, e], out.at[pl.ds(nb + e * ns, ns)], loc.at[3]),
+            pltpu.make_async_copy(ra.at[:, s], out.at[0, :, s], loc.at[2]),
+            pltpu.make_async_copy(rb.at[:, e], out.at[1, e], loc.at[3]),
         ]
 
         def begin():
@@ -346,18 +349,6 @@
 
         return begin, middle, end
 
-    begin, middle, end = exchange(
-        f_a,
-        f_b,
-        f_ra,
-        f_rb,
-        f_in,
-        (fa1_send, fa1_recv, fa2_send, fa2_recv, fb1_send, fb1_recv, fb2_send, fb2_recv),
-        f_loc,
-    )
-    begin()
-
-    tiles_y = LANES // rows_t
     half_rows = tiles_y * rows_b
     pick_b = jnp.where(iota((half_rows, rows_b), 0) % rows_b == iota((half_rows, rows_b), 1), 1.0, 0.0)
     pick_y = jnp.where(iota((rows_t, LANES), 1) % rows_t == iota((rows_t, LANES), 0), 1.0, 0.0)
@@ -388,75 +379,54 @@
         return along_z[:ny] + along_y[:, :LANES], along_z[ny:] + along_y[:, LANES:]
 
     def stencil(buf, x):
-        total = coeffs[0, x, 0] * buf[x]
+        total = coeffs[0, 0, x] * buf[x]
         for k in range(1, 2 * reach + 1):
-            total = total + coeffs[0, x, k] * buf[x + k]
+            total = total + coeffs[k, 0, x] * buf[x + k]
         return total
 
     pairs = planes // 2
     edge = reach // 2
 
-    def over_planes(body, before_edges):
+    def over_interior(body):
         def interior(i, carry):
             body(2 * i)
             return carry
 
-        lax.fori_loop(edge, pairs - edge, interior, 0)
-        before_edges()
-
-        def edges(i, carry):
-            body(2 * jnp.where(i < edge, i, pairs - 2 * edge + i))
+        lax.fori_loop(edge, pairs - edge, interior, 0, unroll=2)
+
+    def over_edge(body, side):
+        start = 0 if side == 0 else pairs - edge
+
+        def one(i, carry):
+            body(2 * i)
             return carry
 
-        lax.fori_loop(0, 2 * edge, edges, 0)
+        lax.fori_loop(start, start + edge, one, 0, unroll=2)
 
     def first_stiff(x):
         for p, part in enumerate(stiff_pair(x)):
             ku0[x + p] = part + stencil(u_a, x + p)
 
-    over_planes(first_stiff, lambda: take_halos(0, u_a))
-    middle()
+    load_coeffs.wait()
+    over_interior(first_stiff)
+    for side in range(2):
+        take_halo(0, side, u_a)
+        over_edge(first_stiff, side)
     f_in[2 * nb] = jnp.zeros(f_in.shape[1:], BF16)
-
-    ids_f = jnp.where(
-        sub == 0,
-        jnp.broadcast_to(asked_0, (ROWS, LANES)),
-        jnp.broadcast_to(asked_1, (ROWS, LANES)),
-    ).astype(F32).astype(BF16)
-
-    slots = ns * ne
-
-    def spread(rank_row, position, base):
-        width = slots * rows_b
-        chunk = min(512, width)
-        for c0 in range(0, width, chunk):
-            lane = iota((LANES, chunk), 1) + c0
-            source = position(lane // rows_b)
-            pick = jnp.where(iota((LANES, chunk), 0) == source, 1.0, 0.0).astype(BF16)
-            key = dot(ids_f, pick)[rank_row : rank_row + 1].astype(I32) * rows_b
-            key = key + (iota((1, chunk), 1) + c0) % rows_b
-            rows = blk * rows_b
-            hot = jnp.where(
-                jnp.broadcast_to(key, (rows, chunk)) == iota((rows, chunk), 0), 1.0, 0.0
-            )
-            one_hot[:, base + c0 : base + c0 + chunk] = hot.astype(BF16)
-
-    spread(0, lambda slot: (slot // ne) * ROWS + slot % ne, 0)
-    spread(1, lambda slot: (slot % ns) * ROWS + slot // ns, slots * rows_b)
-
     own_copy.wait()
     load_back.wait()
     load_prev.wait()
-    end()
+    for c in fetches:
+        c.wait()
 
     def take_tile(i, carry):
-        tiles[i] = f_in[own_sm[0, i]]
+        for q in range(tiles_y):
+            tiles[i * tiles_y + q] = f_in[own_sm[0, q * planes + i]]
         return carry
 
-    lax.fori_loop(0, n_tiles, take_tile, 0, unroll=8)
-
-    def speed_pair(i, carry):
-        x = 2 * i
+    lax.fori_loop(0, planes, take_tile, 0, unroll=2)
+
+    def speed_pair(x):
         blocks = tiles[pl.ds(x * tiles_y, 2 * tiles_y)].reshape(2 * half_rows, LANES)
         high, low = split(dot(blocks, interp_z[...]))
         right = jnp.concatenate(
@@ -467,38 +437,37 @@
             axis=0,
         )
         perturb = dot(w_fwd[...], right)
-        speed[x] = speed[x] * jnp.exp(perturb[:, :LANES])
-        speed[x + 1] = speed[x + 1] * jnp.exp(perturb[:, LANES:])
-        return carry
-
-    lax.fori_loop(0, pairs, speed_pair, 0)
+        for p in range(2):
+            speed[x + p] = speed[x + p] * jnp.exp(perturb[:, p * LANES : (p + 1) * LANES])
 
     def advance(x, force, step, now, prev):
         change = speed[x] * force
         drawn = adj[step, x] * change
+        if step == steps - 1:
+            ku0[x] = change
+            u_hl[x, 1] = (kern[x] - drawn).astype(BF16)
+            return
         if step == 0:
             kern[x] = -drawn
-        elif step < steps - 1:
+        else:
             kern[x] = kern[x] - drawn
-        else:
-            total = (kern[x] - drawn).astype(BF16)
-            u_hl[x, 1] = total
         later = 2.0 * now[x + reach] - prev[x + reach] - change
         prev[x + reach] = later
-        if step < steps - 1:
-            high, low = split(later)
-            u_hl[x, 0] = high
-            u_hl[x, 1] = low
+        high, low = split(later)
+        u_hl[x, 0] = high
+        u_hl[x, 1] = low
 
     load_adj[0].wait()
 
-    def first_step(i, carry):
-        advance(i, ku0[i], 0, u_a, u_b)
-        return carry
-
-    lax.fori_loop(0, planes, first_step, 0)
-    if steps > 1:
-        send_halos(1)
+    def first_step(x):
+        speed_pair(x)
+        for p in range(2):
+            advance(x + p, ku0[x + p], 0, u_a, u_b)
+
+    for side in range(2):
+        over_edge(first_step, side)
+        send_halo(1, side)
+    over_interior(first_step)
     now, prev = u_b, u_a
     for step in range(1, steps):
         load_adj[step].wait()
@@ -508,13 +477,15 @@
             for p in range(2):
                 advance(x + p, parts[p] + stencil(now, x + p), step, now, prev)
 
-        over_planes(body, functools.partial(take_halos, step, now))
-        if step < steps - 1:
-            send_halos(step + 1)
+        over_interior(body)
+        for i in range(2):
+            side = (step + i) % 2
+            take_halo(step, side, now)
+            over_edge(body, side)
+            if step < steps - 1:
+                send_halo(step + 1, side)
         now, prev = prev, now
-
-    wave_copy = pltpu.make_async_copy(now.at[pl.ds(reach, planes)], wave_out.at[0], out_sem)
-    wave_copy.start()
+    now, prev = prev, now
 
     def grad_pair(i, carry):
         x = 2 * i
@@ -530,7 +501,7 @@
         )
         return carry
 
-    lax.fori_loop(0, pairs, grad_pair, 0)
+    lax.fori_loop(0, pairs, grad_pair, 0, unroll=4)
     g_tiles[n_tiles] = jnp.zeros(g_tiles.shape[1:], BF16)
 
     def pack(i, carry):
@@ -550,7 +521,39 @@
         g_loc,
     )
     begin()
+
+    def last_wave(i, carry):
+        prev[reach + i] = 2.0 * now[reach + i] - prev[reach + i] - ku0[i]
+        return carry
+
+    lax.fori_loop(0, planes, last_wave, 0)
+    wave_copy = pltpu.make_async_copy(prev.at[pl.ds(reach, planes)], wave_out.at[0], out_sem)
+    wave_copy.start()
     middle()
+
+    for c in ask_copies:
+        c.wait()
+    ranks = []
+    for r in range(2):
+        table = jnp.zeros((ROWS, LANES), I32)
+        for i in range(ne):
+            table = jnp.where(
+                sub == i, jnp.broadcast_to(asked_all[i][r : r + 1], (ROWS, LANES)), table
+            )
+        ranks.append(table)
+    width = ns * rows_b
+    lane = iota((LANES, width), 1)
+    pick = jnp.where(iota((LANES, width), 0) == lane // rows_b * ROWS + e, 1.0, 0.0)
+    asked_both = jnp.concatenate(ranks, axis=0).astype(F32).astype(BF16)
+    keys = dot(asked_both, pick.astype(BF16)).astype(I32) * rows_b
+    keys = keys + iota((2 * ROWS, width), 1) % rows_b
+    rows = iota((blk * rows_b, width), 0)
+    for r in range(2):
+        for i in range(ne):
+            key = keys[r * ROWS + i : r * ROWS + i + 1]
+            hot = jnp.where(jnp.broadcast_to(key, rows.shape) == rows, 1.0, 0.0)
+            at = (r * ne + i) * width
+            one_hot[:, at : at + width] = hot.astype(BF16)
     end()
     received = g_in[...].reshape(2 * nb * rows_b, LANES)
     total = dot(one_hot[...], received)
@@ -586,9 +589,8 @@
     tiles_y = block_index.shape[2]
     n_tiles = planes * tiles_y
     rows_t = ny // tiles_y
-    ids = block_index.reshape(1, n_tiles)
-    if n_tiles < LANES:
-        ids = jnp.pad(ids, ((0, 0), (0, LANES - n_tiles)), constant_values=-1)
+    ids = jnp.swapaxes(block_index, 1, 2)
+    coeffs = jnp.transpose(coeffs_x, (2, 0, 1))
     cfg = (ne, ns, planes, reach, steps, n_tiles, rows_t, blk, rows_b)
     dma = pltpu.SemaphoreType.DMA
     vmem = pltpu.VMEM
@@ -605,7 +607,6 @@
     def sems():
         return [dma((n,)) for n in (ne, ne, ns, ns, ns, ns, ne, ne)] + [dma((4,))]
 
-    fetch = buffers()
     grads = buffers()
     whole = pl.BlockSpec(memory_space=pltpu.VMEM)
     smem = pl.BlockSpec(memory_space=pltpu.SMEM)
@@ -616,7 +617,7 @@
             jax.ShapeDtypeStruct(wave_now.shape, F32),
             jax.ShapeDtypeStruct(model.shape, F32),
         ),
-        in_specs=[hbm] * 4 + [smem] * 2 + [whole] * 6,
+        in_specs=[hbm] * 5 + [smem] + [whole] * 6,
         out_specs=(hbm, whole),
         scratch_shapes=[
             vmem((planes + 2 * reach, ny, nz), F32),
@@ -632,29 +633,35 @@
             vmem((ny, 2 * tiles_y * rows_b), BF16),
             vmem((tiles_y * rows_b, ny), BF16),
             vmem((2 * nz, nz), BF16),
-            vmem((ne, ROWS, LANES), I32),
+            pltpu.SMEM(coeffs.shape, F32),
             vmem((ROWS, LANES), I32),
             vmem((LANES // ROWS, ROWS, LANES), I32),
             vmem((ROWS, LANES), I32),
             vmem((ROWS, LANES), I32),
+            vmem((ne, ROWS, LANES), I32),
             pltpu.SMEM((ROWS, LANES), I32),
             pltpu.SMEM((ROWS, LANES), I32),
-            *fetch,
+            vmem((ne,) + model.shape, BF16),
+            vmem((ns, 2 * ne) + slot, BF16),
             vmem((2 * nb + 1,) + slot, BF16),
             vmem((n_tiles,) + slot, BF16),
             vmem((n_tiles + 1,) + slot, BF16),
             *grads,
-            vmem((2 * nb,) + slot, BF16),
+            vmem((2, ne, ns) + slot, BF16),
             vmem((blk * rows_b, 2 * nb * rows_b), BF16),
             dma((3 + steps,)),
-            dma((2,)),
+            dma((3,)),
+            dma((ns,)),
+            dma((ns,)),
+            dma((ne,)),
+            dma((ne,)),
             dma((ne,)),
             dma((ne,)),
             dma((ns,)),
             dma((ns,)),
             dma((steps, 2)),
             dma((steps, 2)),
-            *sems(),
+            dma,
             *sems(),
             dma,
         ],
@@ -667,7 +674,7 @@
         wave_now,
         adjoint,
         background,
-        coeffs_x,
+        coeffs,
         live_count,
         stiff_y,
         stiff_z,

time: 92.9 us -> 77.9 us (0.84)
  Pallas kernels: 84.7 us -> 72.6 us
  local copies, waits for them, and re-layouts: 6.58 us -> 3.83 us
    pallas_call x1, Pallas kernels: 84.7 us -> 72.6 us  [shards(): pl.pallas_call(functools.partial(window_kernel, cfg), out_shape=(jax.Shap...]
    unnamed x6 -> x4, local copies, waits for them, and re-layouts: 5.96 us -> 3.83 us
where the time goes in v2:
time: 77.9 us; the launch traced here: 77.7 us
  Pallas kernels  72.6 us (93%)
  local copies, waits for them, and re-layouts  3.83 us (5%)
  between operations  1.3 us (2%)
    pallas_call x1, Pallas kernels, shards(): pl.pallas_call(functools.partial(window_kernel, cfg), out_shape=(jax.Shap...  72.6 us
    unnamed x4, local copies, waits for them, and re-layouts  3.83 us

profile of v2, /device:TPU:1, one launch (start us, length us, event | category | flops | bytes accessed | tf_op | source)
XLA Modules:
  0.0 77.7 jit_solution(4768915391494992199)
XLA Ops:
  1.3 72.6 %window.1 = (f32[1,32,128,128]{3,2,1,0:T(8,128)}, f32[16,16,128]{2,1,0:T(8,128)}) custom-call(f32[1,32,128,128]{3,2,1,0:T(8,128)} %prev_hbm.1, f32[1,32,128,128]{3,2,1,0:T(8,128)} %now_hbm.1, f32[1,4,32,128,128]{4,3,2,1,0:T(8,128)} %adj_hbm.1, f32[1,32,128,128]{3,2,1,0:T(8,128)} %back_hbm.1, f32[9,1,32]{2,1,0:T(1,128)} %bitcast.2, s32[1,1]{1,0:T(1,128)S(6)} %copy.16.live, ...), custom_call_target="tpu_custom_call" | custom-call | tf_op jit(solution)/shard_map/window/pallas_call | solution.py:614
  73.9 0.0 copy-start
  73.9 3.2 %copy.17 = f32[1,32,128,128]{3,2,1,0:T(8,128)} copy(f32[1,32,128,128]{3,2,1,0:T(8,128)} %get-tuple-element.4) | data formatting | bytes 4194304
  77.1 0.0 copy-done
  77.1 0.7 copy.18
Async XLA Ops:
  73.9 3.2 %copy-start = (f32[16,16,128]{2,1,0:T(8,128)S(1)}, f32[16,16,128]{2,1,0:T(8,128)}, u32[]{:S(2)}) copy-start(f32[16,16,128]{2,1,0:T(8,128)} %get-tuple-element.5) | copy-start | bytes 393220

commit v3 on v2

--- a/solution.py
+++ b/solution.py
@@ -1,4 +1,5 @@
 import functools
+import math
 
 import jax
 import jax.numpy as jnp
@@ -37,12 +38,12 @@
     back_hbm,
     coeffs_hbm,
     live,
-    stiff_y,
-    stiff_z,
-    interp_y,
-    interp_z,
+    stiff_y_hbm,
+    stiff_z_hbm,
+    interp_y_hbm,
+    interp_z_hbm,
     model,
-    ids_in,
+    ids_hbm,
     wave_out,
     grad_out,
     u_a,
@@ -59,6 +60,11 @@
     w_bwd,
     w_iz,
     coeffs,
+    stiff_y,
+    stiff_z,
+    interp_y,
+    interp_z,
+    ids_in,
     id_own,
     id_all,
     idx_own,
@@ -78,11 +84,14 @@
     g_in,
     one_hot,
     load_sem,
+    small_sem,
     idx_sem,
     id_send,
     id_recv,
     col_send,
     col_recv,
+    pair_send,
+    pair_recv,
     ask_send,
     ask_recv,
     f_send,
@@ -114,29 +123,58 @@
         pltpu.make_async_copy(adj_hbm.at[0, i], adj.at[i], load_sem.at[3 + i]) for i in range(steps)
     ]
     load_coeffs = pltpu.make_async_copy(coeffs_hbm, coeffs, idx_sem.at[2])
+    load_ids = pltpu.make_async_copy(ids_hbm, ids_in, small_sem.at[0])
+    load_model = pltpu.make_async_copy(model, column.at[e], small_sem.at[1])
+    load_weights = [
+        pltpu.make_async_copy(stiff_y_hbm, stiff_y, small_sem.at[2]),
+        pltpu.make_async_copy(stiff_z_hbm, stiff_z, small_sem.at[3]),
+        pltpu.make_async_copy(interp_y_hbm, interp_y, small_sem.at[4]),
+        pltpu.make_async_copy(interp_z_hbm, interp_z, small_sem.at[5]),
+    ]
+    load_ids.start()
+    load_model.start()
+
+    nz = ne // 2
+    side_len = math.isqrt(ns)
+    z, core = e // 2, lax.rem(e, 2)
+    row, col = s // side_len, lax.rem(s, side_len)
+
+    def event_at(d):
+        return lax.rem(z + d // 2, nz) * 2 + lax.rem(core + d % 2, 2)
+
+    def slab_at(d):
+        y = lax.rem(row + d // side_len, side_len)
+        return y * side_len + lax.rem(col + d % side_len, side_len)
+
+    def around(d, n):
+        return min(d, n - d)
+
+    event_order = sorted(range(1, ne), key=lambda d: -around(d // 2, nz))
+    slab_order = sorted(
+        range(1, ns),
+        key=lambda d: -around(d // side_len, side_len) - around(d % side_len, side_len),
+    )
+
+    barrier = pltpu.get_barrier_semaphore()
+    for d in slab_order:
+        pl.semaphore_signal(barrier, inc=1, device_id=(e, slab_at(d)), device_id_type=MESH)
+    for d in event_order:
+        pl.semaphore_signal(barrier, inc=1, device_id=(event_at(d), s), device_id_type=MESH)
     load_now.start()
+    for c in load_weights:
+        c.start()
     load_coeffs.start()
+    load_back.start()
     load_prev.start()
-    load_back.start()
-
-    barrier = pltpu.get_barrier_semaphore()
-    for d in range(1, ne):
-        pl.semaphore_signal(
-            barrier, inc=1, device_id=(lax.rem(e + d, ne), s), device_id_type=MESH
-        )
-    for d in range(1, ns):
-        pl.semaphore_signal(
-            barrier, inc=1, device_id=(e, lax.rem(s + d, ns)), device_id_type=MESH
-        )
-    pl.semaphore_wait(barrier, ne - 1 + ns - 1)
-
-    def event_copy(src, dst, send, recv, d):
+
+    def event_copy(src, dst, send, recv, d, at=None):
+        at = d if at is None else at
         return pltpu.make_async_remote_copy(
             src_ref=src,
             dst_ref=dst,
-            send_sem=send.at[d],
-            recv_sem=recv.at[d],
-            device_id=(lax.rem(e + d, ne), s),
+            send_sem=send.at[at],
+            recv_sem=recv.at[at],
+            device_id=(event_at(d), s),
             device_id_type=MESH,
         )
 
@@ -146,11 +184,19 @@
             dst_ref=dst,
             send_sem=send.at[d],
             recv_sem=recv.at[d],
-            device_id=(e, lax.rem(s + d, ns)),
+            device_id=(e, slab_at(d)),
             device_id_type=MESH,
         )
 
-    column_copies = [event_copy(model, column.at[e], col_send, col_recv, d) for d in range(1, ne)]
+    far = [
+        event_copy(column.at[e], column.at[e], col_send, col_recv, 2 * d) for d in range(1, nz)
+    ]
+    mine = [event_at(2 * ((nz - d) % nz)) for d in range(nz)]
+    near = [
+        event_copy(column.at[mine[d]], column.at[mine[d]], pair_send, pair_recv, 1, d)
+        for d in range(nz)
+    ]
+    load_ids.wait()
     sub = iota((ROWS, LANES), 0)
     planes_id = ids_in[0]
     ids_row = jnp.concatenate([planes_id[q : q + 1] for q in range(tiles_y)], axis=1)
@@ -162,12 +208,14 @@
         if i >= ns:
             id_all[i] = jnp.full((ROWS, LANES), -1, I32)
     id_all[s] = ids
-    id_copies = [slab_copy(id_own, id_all.at[s], id_send, id_recv, d) for d in range(1, ns)]
+    pl.semaphore_wait(barrier, ne - 1 + ns - 1)
+    id_copies = [slab_copy(id_own, id_all.at[s], id_send, id_recv, d) for d in slab_order]
     for c in id_copies:
         c.start()
-    for c in column_copies:
+    load_model.wait()
+    for c in far[::-1]:
         c.start()
-    column[e] = model[...]
+    near[0].start()
     for c in load_adj:
         c.start()
 
@@ -214,6 +262,8 @@
     own_copy = pltpu.make_async_copy(idx_own, own_sm, idx_sem.at[0])
     own_copy.start()
 
+    for c in load_weights:
+        c.wait()
     high, low = split(stiff_y[...])
     w_y[...] = jnp.concatenate(
         [jnp.concatenate([high, high], axis=1), jnp.concatenate([low, low], axis=1)], axis=0
@@ -258,6 +308,9 @@
     lax.fori_loop(planes - reach, planes, split_planes, 0, unroll=2)
     send_halo(0, 0)
     send_halo(0, 1)
+    for d in range(1, nz):
+        far[d - 1].wait_recv()
+        near[d].start()
     lax.fori_loop(reach, planes - reach, split_planes, 0, unroll=2)
     zero_halo = jnp.zeros((reach,) + u_a.shape[1:], F32)
     for buf in (u_a, u_b):
@@ -265,14 +318,14 @@
         buf[pl.ds(reach + planes, reach)] = zero_halo
 
     for c in id_copies:
-        c.wait()
+        c.wait_recv()
     asked_ids = id_all[...].reshape(LANES, LANES)
     wanted = (row_i % ROWS) * ns + s
-    mine = (lax.shift_right_arithmetic(asked_ids, cfg_shift(blk)) == wanted) & (row_i % ROWS < ne)
+    asks = (lax.shift_right_arithmetic(asked_ids, cfg_shift(blk)) == wanted) & (row_i % ROWS < ne)
     code = lane_i * blk + (asked_ids & (blk - 1))
     none = LANES * blk
-    code_0 = jnp.min(jnp.where(mine, code, none), axis=1, keepdims=True)
-    code_1 = jnp.min(jnp.where(mine & (code > code_0), code, none), axis=1, keepdims=True)
+    code_0 = jnp.min(jnp.where(asks, code, none), axis=1, keepdims=True)
+    code_1 = jnp.min(jnp.where(asks & (code > code_0), code, none), axis=1, keepdims=True)
     asked_0 = as_row(code_0) & (blk - 1)
     asked_1 = as_row(code_1) & (blk - 1)
     asked = jnp.where(
@@ -284,12 +337,12 @@
     req_copy = pltpu.make_async_copy(idx_req, req_sm, idx_sem.at[1])
     req_copy.start()
     asked_all[e] = asked
-    for c in column_copies:
-        c.wait()
+    for c in near:
+        c.wait_recv()
     req_copy.wait()
     fetches = []
-    for d in [*range(1, ns), 0]:
-        to = lax.rem(s + d, ns)
+    for d in slab_order + [0]:
+        to = slab_at(d)
         for j in range(ne):
             f_out[to, j] = column[j, req_sm[0, to * ROWS + j]]
             f_out[to, ne + j] = column[j, req_sm[1, to * ROWS + j]]
@@ -301,53 +354,12 @@
         c.start()
         fetches.append(c)
     ask_copies = [
-        event_copy(idx_req, asked_all.at[e], ask_send, ask_recv, d) for d in range(1, ne)
+        event_copy(idx_req, asked_all.at[e], ask_send, ask_recv, d) for d in event_order
     ]
     for c in ask_copies:
         c.start()
-
-    def exchange(a, b, ra, rb, out, sems, loc):
-        a1s, a1r, a2s, a2r, b1s, b1r, b2s, b2r = sems
-        a1 = [
-            event_copy(a.at[lax.rem(e + d, ne)], ra.at[e], a1s, a1r, d) for d in range(1, ne)
-        ]
-        b1 = [slab_copy(b.at[lax.rem(s + d, ns)], rb.at[s], b1s, b1r, d) for d in range(1, ns)]
-        here = [
-            pltpu.make_async_copy(a.at[e], ra.at[e], loc.at[0]),
-            pltpu.make_async_copy(b.at[s], rb.at[s], loc.at[1]),
-        ]
-        a2 = [
-            slab_copy(ra.at[:, lax.rem(s + d, ns)], out.at[0, :, s], a2s, a2r, d)
-            for d in range(1, ns)
-        ]
-        b2 = [
-            event_copy(rb.at[:, lax.rem(e + d, ne)], out.at[1, e], b2s, b2r, d)
-            for d in range(1, ne)
-        ]
-        there = [
-            pltpu.make_async_copy(ra.at[:, s], out.at[0, :, s], loc.at[2]),
-            pltpu.make_async_copy(rb.at[:, e], out.at[1, e], loc.at[3]),
-        ]
-
-        def begin():
-            for c in a1 + b1 + here:
-                c.start()
-
-        def middle():
-            for c in here[:1] + a1:
-                c.wait()
-            for c in a2 + there[:1]:
-                c.start()
-            for c in here[1:] + b1:
-                c.wait()
-            for c in b2 + there[1:]:
-                c.start()
-
-        def end():
-            for c in a2 + b2 + there:
-                c.wait()
-
-        return begin, middle, end
+    for c in id_copies + far + near:
+        c.wait_send()
 
     half_rows = tiles_y * rows_b
     pick_b = jnp.where(iota((half_rows, rows_b), 0) % rows_b == iota((half_rows, rows_b), 1), 1.0, 0.0)
@@ -416,8 +428,11 @@
     own_copy.wait()
     load_back.wait()
     load_prev.wait()
-    for c in fetches:
-        c.wait()
+    for c in fetches[:-1]:
+        c.wait_recv()
+    for c in fetches[:-1]:
+        c.wait_send()
+    fetches[-1].wait()
 
     def take_tile(i, carry):
         for q in range(tiles_y):
@@ -504,23 +519,48 @@
     lax.fori_loop(0, pairs, grad_pair, 0, unroll=4)
     g_tiles[n_tiles] = jnp.zeros(g_tiles.shape[1:], BF16)
 
-    def pack(i, carry):
+    def pack_event(d):
+        to = event_at(d)
+
+        def one(i, carry):
+            g_a[to, i] = g_tiles[own_sm[1, to * ns + i]]
+            return carry
+
+        lax.fori_loop(0, ns, one, 0, unroll=ns)
+        if d == 0:
+            return pltpu.make_async_copy(g_a.at[to], g_ra.at[e], g_loc.at[0])
+        return event_copy(g_a.at[to], g_ra.at[e], ga1_send, ga1_recv, d)
+
+    def pack_slab(d):
+        to = slab_at(d)
         for j in range(ne):
-            g_a[j, i] = g_tiles[own_sm[1, j * ns + i]]
-            g_b[i, j] = g_tiles[own_sm[2, j * ns + i]]
-        return carry
-
-    lax.fori_loop(0, ns, pack, 0)
-    begin, middle, end = exchange(
-        g_a,
-        g_b,
-        g_ra,
-        g_rb,
-        g_in,
-        (ga1_send, ga1_recv, ga2_send, ga2_recv, gb1_send, gb1_recv, gb2_send, gb2_recv),
-        g_loc,
-    )
-    begin()
+            g_b[to, j] = g_tiles[own_sm[2, j * ns + to]]
+        if d == 0:
+            return pltpu.make_async_copy(g_b.at[to], g_rb.at[s], g_loc.at[1])
+        return slab_copy(g_b.at[to], g_rb.at[s], gb1_send, gb1_recv, d)
+
+    a1, b1 = [], []
+    events, slabs = event_order + [0], slab_order + [0]
+    for i in range(max(ne, ns // 2)):
+        for d in slabs[2 * i : 2 * i + 2]:
+            b1.append(pack_slab(d))
+            b1[-1].start()
+        for d in events[i : i + 1]:
+            a1.append(pack_event(d))
+            a1[-1].start()
+    a2 = [
+        slab_copy(g_ra.at[:, slab_at(d)], g_in.at[0, :, s], ga2_send, ga2_recv, d)
+        for d in slab_order
+    ] + [pltpu.make_async_copy(g_ra.at[:, s], g_in.at[0, :, s], g_loc.at[2])]
+    b2 = [
+        event_copy(g_rb.at[:, event_at(d)], g_in.at[1, e], gb2_send, gb2_recv, d)
+        for d in event_order
+    ] + [pltpu.make_async_copy(g_rb.at[:, e], g_in.at[1, e], g_loc.at[3])]
+
+    def arrive(copies):
+        for c in copies[:-1]:
+            c.wait_recv()
+        copies[-1].wait()
 
     def last_wave(i, carry):
         prev[reach + i] = 2.0 * now[reach + i] - prev[reach + i] - ku0[i]
@@ -529,10 +569,15 @@
     lax.fori_loop(0, planes, last_wave, 0)
     wave_copy = pltpu.make_async_copy(prev.at[pl.ds(reach, planes)], wave_out.at[0], out_sem)
     wave_copy.start()
-    middle()
+    arrive(a1)
+    for c in a2:
+        c.start()
+    arrive(b1)
+    for c in b2:
+        c.start()
 
     for c in ask_copies:
-        c.wait()
+        c.wait_recv()
     ranks = []
     for r in range(2):
         table = jnp.zeros((ROWS, LANES), I32)
@@ -554,10 +599,14 @@
             hot = jnp.where(jnp.broadcast_to(key, rows.shape) == rows, 1.0, 0.0)
             at = (r * ne + i) * width
             one_hot[:, at : at + width] = hot.astype(BF16)
-    end()
-    received = g_in[...].reshape(2 * nb * rows_b, LANES)
-    total = dot(one_hot[...], received)
+    half_slots = nb * rows_b
+    arrive(a2)
+    total = dot(one_hot[:, :half_slots], g_in[0].reshape(half_slots, LANES))
+    arrive(b2)
+    total = total + dot(one_hot[:, half_slots:], g_in[1].reshape(half_slots, LANES))
     grad_out[...] = total.reshape(grad_out.shape)
+    for c in a1[:-1] + b1[:-1] + a2[:-1] + b2[:-1] + ask_copies:
+        c.wait_send()
     wave_copy.wait()
 
 
@@ -592,6 +641,23 @@
     ids = jnp.swapaxes(block_index, 1, 2)
     coeffs = jnp.transpose(coeffs_x, (2, 0, 1))
     cfg = (ne, ns, planes, reach, steps, n_tiles, rows_t, blk, rows_b)
+    arrays = (
+        wave_prev,
+        wave_now,
+        adjoint,
+        background,
+        coeffs,
+        live_count,
+        stiff_y,
+        stiff_z,
+        interp_y,
+        interp_z,
+        model,
+        ids,
+    )
+    arrays = [
+        a if a is live_count else pltpu.with_memory_space_constraint(a, pltpu.HBM) for a in arrays
+    ]
     dma = pltpu.SemaphoreType.DMA
     vmem = pltpu.VMEM
     slot = (rows_b, nz)
@@ -610,15 +676,16 @@
     grads = buffers()
     whole = pl.BlockSpec(memory_space=pltpu.VMEM)
     smem = pl.BlockSpec(memory_space=pltpu.SMEM)
-    hbm = pl.BlockSpec(memory_space=pl.ANY)
+    hbm = pl.BlockSpec(memory_space=pltpu.HBM)
+    free = pl.BlockSpec(memory_space=pl.ANY)
     wave, grad = pl.pallas_call(
         functools.partial(window_kernel, cfg),
         out_shape=(
             jax.ShapeDtypeStruct(wave_now.shape, F32),
             jax.ShapeDtypeStruct(model.shape, F32),
         ),
-        in_specs=[hbm] * 5 + [smem] + [whole] * 6,
-        out_specs=(hbm, whole),
+        in_specs=[hbm] * 5 + [smem] + [hbm] * 6,
+        out_specs=(free, whole),
         scratch_shapes=[
             vmem((planes + 2 * reach, ny, nz), F32),
             vmem((planes + 2 * reach, ny, nz), F32),
@@ -634,6 +701,11 @@
             vmem((tiles_y * rows_b, ny), BF16),
             vmem((2 * nz, nz), BF16),
             pltpu.SMEM(coeffs.shape, F32),
+            vmem(stiff_y.shape, F32),
+            vmem(stiff_z.shape, F32),
+            vmem(interp_y.shape, BF16),
+            vmem(interp_z.shape, BF16),
+            vmem(ids.shape, I32),
             vmem((ROWS, LANES), I32),
             vmem((LANES // ROWS, ROWS, LANES), I32),
             vmem((ROWS, LANES), I32),
@@ -650,11 +722,14 @@
             vmem((2, ne, ns) + slot, BF16),
             vmem((blk * rows_b, 2 * nb * rows_b), BF16),
             dma((3 + steps,)),
+            dma((6,)),
             dma((3,)),
             dma((ns,)),
             dma((ns,)),
             dma((ne,)),
             dma((ne,)),
+            dma((ne // 2,)),
+            dma((ne // 2,)),
             dma((ne,)),
             dma((ne,)),
             dma((ns,)),
@@ -666,23 +741,10 @@
             dma,
         ],
         compiler_params=pltpu.CompilerParams(
-            collective_id=0, has_side_effects=True, vmem_limit_bytes=56 * 1024 * 1024
+            collective_id=0, has_side_effects=True, vmem_limit_bytes=40 * 1024 * 1024
         ),
         name="window",
-    )(
-        wave_prev,
-        wave_now,
-        adjoint,
-        background,
-        coeffs,
-        live_count,
-        stiff_y,
-        stiff_z,
-        interp_y,
-        interp_z,
-        model,
-        ids,
-    )
+    )(*arrays)
     return wave, grad
 
 

time: 77.9 us -> 69.3 us (0.89)
  Pallas kernels: 72.6 us -> 65.9 us
  local copies, waits for them, and re-layouts: 3.83 us -> 1.98 us
    pallas_call x1, Pallas kernels: 72.6 us -> 65.9 us  [shards(): pl.pallas_call(functools.partial(window_kernel, cfg), out_shape=(jax.Shap...]
    unnamed x4 -> x2, local copies, waits for them, and re-layouts: 3.83 us -> 1.98 us
where the time goes in v3:
time: 69.3 us; the launch traced here: 69.2 us
  Pallas kernels  65.9 us (95%)
  local copies, waits for them, and re-layouts  1.98 us (3%)
  between operations  1.29 us (2%)
    pallas_call x1, Pallas kernels, shards(): pl.pallas_call(functools.partial(window_kernel, cfg), out_shape=(jax.Shap...  65.9 us
    unnamed x2, local copies, waits for them, and re-layouts  1.98 us

profile of v3, /device:TPU:1, one launch (start us, length us, event | category | flops | bytes accessed | tf_op | source)
XLA Modules:
  0.0 69.2 jit_solution(16210590101941571538)
XLA Ops:
  1.3 65.9 %window.1 = (f32[1,32,128,128]{3,2,1,0:T(8,128)S(1)}, f32[16,16,128]{2,1,0:T(8,128)S(1)}) custom-call(f32[1,32,128,128]{3,2,1,0:T(8,128)} %prev_hbm.1, f32[1,32,128,128]{3,2,1,0:T(8,128)} %now_hbm.1, f32[1,4,32,128,128]{4,3,2,1,0:T(8,128)} %adj_hbm.1, f32[1,32,128,128]{3,2,1,0:T(8,128)} %back_hbm.1, f32[9,1,32]{2,1,0:T(1,128)} %bitcast.2, ...), custom_call_target="tpu_custom_call" | custom-call | tf_op jit(solution)/shard_map/window/pallas_call | solution.py:681
  67.2 1.3 %copy.17 = f32[1,32,128,128]{3,2,1,0:T(8,128)} copy(f32[1,32,128,128]{3,2,1,0:T(8,128)S(1)} %get-tuple-element.4) | data formatting | bytes 4194304
  68.6 0.7 copy.18

commit v4 on v3

--- a/solution.py
+++ b/solution.py
@@ -75,7 +75,6 @@
     column,
     f_out,
     f_in,
-    tiles,
     g_tiles,
     g_a,
     g_b,
@@ -296,13 +295,11 @@
         def _():
             halo_copy(step, side).start()
 
-    def take_halo(step, side, buf):
+    def take_halo(step, side):
         @pl.when(s > 0 if side == 0 else s < ns - 1)
         def _():
             halo_copy(step, side).wait_send()
             halo_copy(step, 1 - side).wait_recv()
-            at = 0 if side == 0 else reach + planes
-            buf[pl.ds(at, reach)] = halo[step, 1 - side].astype(F32)
 
     lax.fori_loop(0, reach, split_planes, 0, unroll=2)
     lax.fori_loop(planes - reach, planes, split_planes, 0, unroll=2)
@@ -312,10 +309,11 @@
         far[d - 1].wait_recv()
         near[d].start()
     lax.fori_loop(reach, planes - reach, split_planes, 0, unroll=2)
-    zero_halo = jnp.zeros((reach,) + u_a.shape[1:], F32)
-    for buf in (u_a, u_b):
-        buf[pl.ds(0, reach)] = zero_halo
-        buf[pl.ds(reach + planes, reach)] = zero_halo
+    for side in range(2):
+
+        @pl.when(s == (0 if side == 0 else ns - 1))
+        def _():
+            halo[:, 1 - side] = jnp.zeros((steps, reach) + u_a.shape[1:], BF16)
 
     for c in id_copies:
         c.wait_recv()
@@ -399,12 +397,15 @@
     pairs = planes // 2
     edge = reach // 2
 
-    def over_interior(body):
+    def over_interior(body, unroll=2):
         def interior(i, carry):
             body(2 * i)
             return carry
 
-        lax.fori_loop(edge, pairs - edge, interior, 0, unroll=2)
+        lax.fori_loop(edge, pairs - edge, interior, 0, unroll=unroll)
+
+    def side_planes(side):
+        return range(reach) if side == 0 else range(planes - reach, planes)
 
     def over_edge(body, side):
         start = 0 if side == 0 else pairs - edge
@@ -415,6 +416,25 @@
 
         lax.fori_loop(start, start + edge, one, 0, unroll=2)
 
+    def own_part(buf, side):
+        for x in side_planes(side)[::2]:
+            for p, part in enumerate(stiff_pair(x)):
+                total = part
+                for k in range(2 * reach + 1):
+                    if 0 <= x + p + k - reach < planes:
+                        total = total + coeffs[k, 0, x + p] * buf[x + p + k]
+                ku0[x + p] = total
+
+    def whole_part(step, x):
+        total = ku0[x]
+        for k in range(2 * reach + 1):
+            at = x + k - reach
+            if at < 0:
+                total = total + coeffs[k, 0, x] * halo[step, 1, at + reach].astype(F32)
+            if at >= planes:
+                total = total + coeffs[k, 0, x] * halo[step, 0, at - planes].astype(F32)
+        return total
+
     def first_stiff(x):
         for p, part in enumerate(stiff_pair(x)):
             ku0[x + p] = part + stencil(u_a, x + p)
@@ -422,8 +442,11 @@
     load_coeffs.wait()
     over_interior(first_stiff)
     for side in range(2):
-        take_halo(0, side, u_a)
-        over_edge(first_stiff, side)
+        own_part(u_a, side)
+    for side in range(2):
+        take_halo(0, side)
+        for x in side_planes(side):
+            ku0[x] = whole_part(0, x)
     f_in[2 * nb] = jnp.zeros(f_in.shape[1:], BF16)
     own_copy.wait()
     load_back.wait()
@@ -434,15 +457,10 @@
         c.wait_send()
     fetches[-1].wait()
 
-    def take_tile(i, carry):
-        for q in range(tiles_y):
-            tiles[i * tiles_y + q] = f_in[own_sm[0, q * planes + i]]
-        return carry
-
-    lax.fori_loop(0, planes, take_tile, 0, unroll=2)
-
     def speed_pair(x):
-        blocks = tiles[pl.ds(x * tiles_y, 2 * tiles_y)].reshape(2 * half_rows, LANES)
+        blocks = jnp.concatenate(
+            [f_in[own_sm[0, q * planes + x + p]] for p in range(2) for q in range(tiles_y)], axis=0
+        )
         high, low = split(dot(blocks, interp_z[...]))
         right = jnp.concatenate(
             [
@@ -454,6 +472,20 @@
         perturb = dot(w_fwd[...], right)
         for p in range(2):
             speed[x + p] = speed[x + p] * jnp.exp(perturb[:, p * LANES : (p + 1) * LANES])
+
+    def grad_pair(x):
+        right = jnp.concatenate([u_hl[x, 1], u_hl[x + 1, 1]], axis=1)
+        back = dot(w_bwd[...], right)
+        parts = []
+        for p in range(2):
+            high, low = split(back[:, p * LANES : (p + 1) * LANES])
+            parts.append(jnp.concatenate([high, low], axis=1))
+        grads = dot(jnp.concatenate(parts, axis=0), w_iz[...])
+        g_tiles[pl.ds(x * tiles_y, 2 * tiles_y)] = grads.astype(BF16).reshape(
+            2 * tiles_y, rows_b, LANES
+        )
+
+    g_tiles[n_tiles] = jnp.zeros(g_tiles.shape[1:], BF16)
 
     def advance(x, force, step, now, prev):
         change = speed[x] * force
@@ -493,31 +525,22 @@
                 advance(x + p, parts[p] + stencil(now, x + p), step, now, prev)
 
         over_interior(body)
+        for side in range(2):
+            own_part(now, side)
+        last = step == steps - 1
+        if last:
+            over_interior(grad_pair, 4)
         for i in range(2):
             side = (step + i) % 2
-            take_halo(step, side, now)
-            over_edge(body, side)
-            if step < steps - 1:
+            take_halo(step, side)
+            for x in side_planes(side):
+                advance(x, whole_part(step, x), step, now, prev)
+            if last:
+                over_edge(grad_pair, side)
+            else:
                 send_halo(step + 1, side)
         now, prev = prev, now
     now, prev = prev, now
-
-    def grad_pair(i, carry):
-        x = 2 * i
-        right = jnp.concatenate([u_hl[x, 1], u_hl[x + 1, 1]], axis=1)
-        back = dot(w_bwd[...], right)
-        parts = []
-        for p in range(2):
-            high, low = split(back[:, p * LANES : (p + 1) * LANES])
-            parts.append(jnp.concatenate([high, low], axis=1))
-        grads = dot(jnp.concatenate(parts, axis=0), w_iz[...])
-        g_tiles[pl.ds(x * tiles_y, 2 * tiles_y)] = grads.astype(BF16).reshape(
-            2 * tiles_y, rows_b, LANES
-        )
-        return carry
-
-    lax.fori_loop(0, pairs, grad_pair, 0, unroll=4)
-    g_tiles[n_tiles] = jnp.zeros(g_tiles.shape[1:], BF16)
 
     def pack_event(d):
         to = event_at(d)
@@ -716,7 +739,6 @@
             vmem((ne,) + model.shape, BF16),
             vmem((ns, 2 * ne) + slot, BF16),
             vmem((2 * nb + 1,) + slot, BF16),
-            vmem((n_tiles,) + slot, BF16),
             vmem((n_tiles + 1,) + slot, BF16),
             *grads,
             vmem((2, ne, ns) + slot, BF16),

time: 69.3 us -> 67.7 us (0.977)
  Pallas kernels: 65.9 us -> 64.3 us
    pallas_call x1, Pallas kernels: 65.9 us -> 64.3 us  [shards(): pl.pallas_call(functools.partial(window_kernel, cfg), out_shape=(jax.Shap...]
where the time goes in v4:
time: 67.7 us; the launch traced here: 67.6 us
  Pallas kernels  64.3 us (95%)
  local copies, waits for them, and re-layouts  1.98 us (3%)
  between operations  1.29 us (2%)
    pallas_call x1, Pallas kernels, shards(): pl.pallas_call(functools.partial(window_kernel, cfg), out_shape=(jax.Shap...  64.3 us
    unnamed x2, local copies, waits for them, and re-layouts  1.98 us

profile of v4, /device:TPU:1, one launch (start us, length us, event | category | flops | bytes accessed | tf_op | source)
XLA Modules:
  0.0 67.6 jit_solution(4304415522900813091)
XLA Ops:
  1.3 64.3 %window.1 = (f32[1,32,128,128]{3,2,1,0:T(8,128)S(1)}, f32[16,16,128]{2,1,0:T(8,128)S(1)}) custom-call(f32[1,32,128,128]{3,2,1,0:T(8,128)} %prev_hbm.1, f32[1,32,128,128]{3,2,1,0:T(8,128)} %now_hbm.1, f32[1,4,32,128,128]{4,3,2,1,0:T(8,128)} %adj_hbm.1, f32[1,32,128,128]{3,2,1,0:T(8,128)} %back_hbm.1, f32[9,1,32]{2,1,0:T(1,128)} %bitcast.2, ...), custom_call_target="tpu_custom_call" | custom-call | tf_op jit(solution)/shard_map/window/pallas_call | solution.py:704
  65.6 1.3 %copy.17 = f32[1,32,128,128]{3,2,1,0:T(8,128)} copy(f32[1,32,128,128]{3,2,1,0:T(8,128)S(1)} %get-tuple-element.4) | data formatting | bytes 4194304
  66.9 0.7 copy.18

commit v5 on v4

--- a/solution.py
+++ b/solution.py
@@ -177,12 +177,13 @@
             device_id_type=MESH,
         )
 
-    def slab_copy(src, dst, send, recv, d):
+    def slab_copy(src, dst, send, recv, d, at=None):
+        at = d if at is None else at
         return pltpu.make_async_remote_copy(
             src_ref=src,
             dst_ref=dst,
-            send_sem=send.at[d],
-            recv_sem=recv.at[d],
+            send_sem=send.at[at],
+            recv_sem=recv.at[at],
             device_id=(e, slab_at(d)),
             device_id_type=MESH,
         )
@@ -397,7 +398,7 @@
     pairs = planes // 2
     edge = reach // 2
 
-    def over_interior(body, unroll=2):
+    def over_interior(body, unroll=6):
         def interior(i, carry):
             body(2 * i)
             return carry
@@ -542,43 +543,52 @@
         now, prev = prev, now
     now, prev = prev, now
 
-    def pack_event(d):
+    events, slabs = event_order + [0], slab_order + [0]
+    chunks = 2
+    many_e, many_s = ne // chunks, ns // chunks
+
+    def pack_event(d, h):
         to = event_at(d)
-
-        def one(i, carry):
-            g_a[to, i] = g_tiles[own_sm[1, to * ns + i]]
-            return carry
-
-        lax.fori_loop(0, ns, one, 0, unroll=ns)
+        part = pl.ds(h * many_s, many_s)
+        for i in range(h * many_s, (h + 1) * many_s):
+            g_a[to, i] = g_tiles[own_sm[1, to * ns + slab_at(slabs[i])]]
+        src, dst = g_a.at[to, part], g_ra.at[e, part]
         if d == 0:
-            return pltpu.make_async_copy(g_a.at[to], g_ra.at[e], g_loc.at[0])
-        return event_copy(g_a.at[to], g_ra.at[e], ga1_send, ga1_recv, d)
-
-    def pack_slab(d):
+            return pltpu.make_async_copy(src, dst, g_loc.at[h])
+        return event_copy(src, dst, ga1_send, ga1_recv, d, h * ne + d)
+
+    def pack_slab(d, h):
         to = slab_at(d)
-        for j in range(ne):
-            g_b[to, j] = g_tiles[own_sm[2, j * ns + to]]
+        part = pl.ds(h * many_e, many_e)
+        for i in range(h * many_e, (h + 1) * many_e):
+            g_b[to, i] = g_tiles[own_sm[2, event_at(events[i]) * ns + to]]
+        src, dst = g_b.at[to, part], g_rb.at[s, part]
         if d == 0:
-            return pltpu.make_async_copy(g_b.at[to], g_rb.at[s], g_loc.at[1])
-        return slab_copy(g_b.at[to], g_rb.at[s], gb1_send, gb1_recv, d)
+            return pltpu.make_async_copy(src, dst, g_loc.at[2 + h])
+        return slab_copy(src, dst, gb1_send, gb1_recv, d, h * ns + d)
 
     a1, b1 = [], []
-    events, slabs = event_order + [0], slab_order + [0]
-    for i in range(max(ne, ns // 2)):
-        for d in slabs[2 * i : 2 * i + 2]:
-            b1.append(pack_slab(d))
-            b1[-1].start()
-        for d in events[i : i + 1]:
-            a1.append(pack_event(d))
-            a1[-1].start()
-    a2 = [
-        slab_copy(g_ra.at[:, slab_at(d)], g_in.at[0, :, s], ga2_send, ga2_recv, d)
-        for d in slab_order
-    ] + [pltpu.make_async_copy(g_ra.at[:, s], g_in.at[0, :, s], g_loc.at[2])]
-    b2 = [
-        event_copy(g_rb.at[:, event_at(d)], g_in.at[1, e], gb2_send, gb2_recv, d)
-        for d in event_order
-    ] + [pltpu.make_async_copy(g_rb.at[:, e], g_in.at[1, e], g_loc.at[3])]
+    for h in range(chunks):
+        a1.append([])
+        b1.append([])
+        for i in range(max(ne, ns // 2)):
+            for d in events[i : i + 1]:
+                a1[h].append(pack_event(d, h))
+                a1[h][-1].start()
+            for d in slabs[2 * i : 2 * i + 2]:
+                b1[h].append(pack_slab(d, h))
+                b1[h][-1].start()
+    a2, b2 = [], []
+    for i, d in enumerate(slabs):
+        if d == 0:
+            a2.append(pltpu.make_async_copy(g_ra.at[:, i], g_in.at[0, :, s], g_loc.at[4]))
+        else:
+            a2.append(slab_copy(g_ra.at[:, i], g_in.at[0, :, s], ga2_send, ga2_recv, d))
+    for i, d in enumerate(events):
+        if d == 0:
+            b2.append(pltpu.make_async_copy(g_rb.at[:, i], g_in.at[1, e], g_loc.at[5]))
+        else:
+            b2.append(event_copy(g_rb.at[:, i], g_in.at[1, e], gb2_send, gb2_recv, d))
 
     def arrive(copies):
         for c in copies[:-1]:
@@ -592,12 +602,13 @@
     lax.fori_loop(0, planes, last_wave, 0)
     wave_copy = pltpu.make_async_copy(prev.at[pl.ds(reach, planes)], wave_out.at[0], out_sem)
     wave_copy.start()
-    arrive(a1)
-    for c in a2:
-        c.start()
-    arrive(b1)
-    for c in b2:
-        c.start()
+    for h in range(chunks):
+        arrive(a1[h])
+        for c in a2[h * many_s : (h + 1) * many_s]:
+            c.start()
+        arrive(b1[h])
+        for c in b2[h * many_e : (h + 1) * many_e]:
+            c.start()
 
     for c in ask_copies:
         c.wait_recv()
@@ -628,7 +639,10 @@
     arrive(b2)
     total = total + dot(one_hot[:, half_slots:], g_in[1].reshape(half_slots, LANES))
     grad_out[...] = total.reshape(grad_out.shape)
-    for c in a1[:-1] + b1[:-1] + a2[:-1] + b2[:-1] + ask_copies:
+    for h in range(chunks):
+        for c in a1[h][:-1] + b1[h][:-1]:
+            c.wait_send()
+    for c in a2[:-1] + b2[:-1] + ask_copies:
         c.wait_send()
     wave_copy.wait()
 
@@ -694,7 +708,7 @@
         ]
 
     def sems():
-        return [dma((n,)) for n in (ne, ne, ns, ns, ns, ns, ne, ne)] + [dma((4,))]
+        return [dma((n,)) for n in (2 * ne, 2 * ne, ns, ns, 2 * ns, 2 * ns, ne, ne)] + [dma((6,))]
 
     grads = buffers()
     whole = pl.BlockSpec(memory_space=pltpu.VMEM)

time: 67.7 us -> 66.2 us (0.978)
  Pallas kernels: 64.3 us -> 62.8 us
    pallas_call x1, Pallas kernels: 64.3 us -> 62.8 us  [shards(): pl.pallas_call(functools.partial(window_kernel, cfg), out_shape=(jax.Shap...]
where the time goes in v5:
time: 66.2 us; the launch traced here: 66.1 us
  Pallas kernels  62.8 us (95%)
  local copies, waits for them, and re-layouts  1.98 us (3%)
  between operations  1.29 us (2%)
    pallas_call x1, Pallas kernels, shards(): pl.pallas_call(functools.partial(window_kernel, cfg), out_shape=(jax.Shap...  62.8 us
    unnamed x2, local copies, waits for them, and re-layouts  1.98 us

profile of v5, /device:TPU:1, one launch (start us, length us, event | category | flops | bytes accessed | tf_op | source)
XLA Modules:
  0.0 66.1 jit_solution(10634996740085086574)
XLA Ops:
  1.3 62.8 %window.1 = (f32[1,32,128,128]{3,2,1,0:T(8,128)S(1)}, f32[16,16,128]{2,1,0:T(8,128)S(1)}) custom-call(f32[1,32,128,128]{3,2,1,0:T(8,128)} %prev_hbm.1, f32[1,32,128,128]{3,2,1,0:T(8,128)} %now_hbm.1, f32[1,4,32,128,128]{4,3,2,1,0:T(8,128)} %adj_hbm.1, f32[1,32,128,128]{3,2,1,0:T(8,128)} %back_hbm.1, f32[9,1,32]{2,1,0:T(1,128)} %bitcast.2, ...), custom_call_target="tpu_custom_call" | custom-call | tf_op jit(solution)/shard_map/window/pallas_call | solution.py:718
  64.1 1.3 %copy.17 = f32[1,32,128,128]{3,2,1,0:T(8,128)} copy(f32[1,32,128,128]{3,2,1,0:T(8,128)S(1)} %get-tuple-element.4) | data formatting | bytes 4194304
  65.4 0.7 copy.18

commit v6 on v5

--- a/solution.py
+++ b/solution.py
@@ -188,6 +188,7 @@
             device_id_type=MESH,
         )
 
+    far_order = sorted(range(1, nz), key=lambda d: -around(d, nz))
     far = [
         event_copy(column.at[e], column.at[e], col_send, col_recv, 2 * d) for d in range(1, nz)
     ]
@@ -210,67 +211,14 @@
     id_all[s] = ids
     pl.semaphore_wait(barrier, ne - 1 + ns - 1)
     id_copies = [slab_copy(id_own, id_all.at[s], id_send, id_recv, d) for d in slab_order]
+    load_model.wait()
+    for d in far_order:
+        far[d - 1].start()
+    near[0].start()
     for c in id_copies:
         c.start()
-    load_model.wait()
-    for c in far[::-1]:
-        c.start()
-    near[0].start()
     for c in load_adj:
         c.start()
-
-    owners = lax.shift_right_arithmetic(jnp.broadcast_to(ids_row, (LANES, LANES)), cfg_shift(blk))
-    owners_t = jnp.transpose(owners)
-    row_i = iota((LANES, LANES), 0)
-    lane_i = iota((LANES, LANES), 1)
-    earlier = jnp.where((owners == owners_t) & (row_i < lane_i), 1, 0)
-    rank = jnp.sum(earlier, axis=0, keepdims=True)
-    owner_row = owners[0:1]
-    at_e = owner_row // ns
-    at_s = owner_row - at_e * ns
-    live_n = live[0, 0]
-
-    def in_order(lane):
-        return lane % planes * tiles_y + lane // planes
-
-    address = at_s * (2 * ne) + rank * ne + at_e
-    alive = in_order(iota((1, LANES), 1)) < live_n
-    address = jnp.where(alive, address, 2 * nb)
-    none = LANES
-    match = owners == row_i
-    first = jnp.min(jnp.where(match, lane_i, none), axis=1, keepdims=True)
-    second = jnp.min(jnp.where(match & (lane_i > first), lane_i, none), axis=1, keepdims=True)
-
-    def as_row(values):
-        return jnp.transpose(jnp.broadcast_to(values, (LANES, LANES)))[0:1]
-
-    def tile_at(lane):
-        tile = in_order(lane)
-        return jnp.where((lane < none) & (tile < live_n), tile, n_tiles)
-
-    tile_0 = tile_at(as_row(first))
-    tile_1 = tile_at(as_row(second))
-    idx_own[...] = jnp.where(
-        sub == 0,
-        jnp.broadcast_to(address, (ROWS, LANES)),
-        jnp.where(
-            sub == 1,
-            jnp.broadcast_to(tile_0, (ROWS, LANES)),
-            jnp.broadcast_to(tile_1, (ROWS, LANES)),
-        ),
-    )
-    own_copy = pltpu.make_async_copy(idx_own, own_sm, idx_sem.at[0])
-    own_copy.start()
-
-    for c in load_weights:
-        c.wait()
-    high, low = split(stiff_y[...])
-    w_y[...] = jnp.concatenate(
-        [jnp.concatenate([high, high], axis=1), jnp.concatenate([low, low], axis=1)], axis=0
-    )
-    high, low = split(jnp.transpose(stiff_z[...]))
-    half = jnp.concatenate([high, low], axis=1)
-    w_z[...] = jnp.concatenate([half, half], axis=0)
 
     load_now.wait()
 
@@ -306,15 +254,14 @@
     lax.fori_loop(planes - reach, planes, split_planes, 0, unroll=2)
     send_halo(0, 0)
     send_halo(0, 1)
-    for d in range(1, nz):
+    for d in far_order[::-1]:
         far[d - 1].wait_recv()
         near[d].start()
-    lax.fori_loop(reach, planes - reach, split_planes, 0, unroll=2)
-    for side in range(2):
-
-        @pl.when(s == (0 if side == 0 else ns - 1))
-        def _():
-            halo[:, 1 - side] = jnp.zeros((steps, reach) + u_a.shape[1:], BF16)
+    row_i = iota((LANES, LANES), 0)
+    lane_i = iota((LANES, LANES), 1)
+
+    def as_row(values):
+        return jnp.transpose(jnp.broadcast_to(values, (LANES, LANES)))[0:1]
 
     for c in id_copies:
         c.wait_recv()
@@ -359,6 +306,61 @@
         c.start()
     for c in id_copies + far + near:
         c.wait_send()
+
+    owners = lax.shift_right_arithmetic(jnp.broadcast_to(ids_row, (LANES, LANES)), cfg_shift(blk))
+    owners_t = jnp.transpose(owners)
+    earlier = jnp.where((owners == owners_t) & (row_i < lane_i), 1, 0)
+    rank = jnp.sum(earlier, axis=0, keepdims=True)
+    owner_row = owners[0:1]
+    at_e = owner_row // ns
+    at_s = owner_row - at_e * ns
+    live_n = live[0, 0]
+
+    def in_order(lane):
+        return lane % planes * tiles_y + lane // planes
+
+    address = at_s * (2 * ne) + rank * ne + at_e
+    alive = in_order(iota((1, LANES), 1)) < live_n
+    address = jnp.where(alive, address, 2 * nb)
+    none = LANES
+    match = owners == row_i
+    first = jnp.min(jnp.where(match, lane_i, none), axis=1, keepdims=True)
+    second = jnp.min(jnp.where(match & (lane_i > first), lane_i, none), axis=1, keepdims=True)
+
+    def tile_at(lane):
+        tile = in_order(lane)
+        return jnp.where((lane < none) & (tile < live_n), tile, n_tiles)
+
+    tile_0 = tile_at(as_row(first))
+    tile_1 = tile_at(as_row(second))
+    idx_own[...] = jnp.where(
+        sub == 0,
+        jnp.broadcast_to(address, (ROWS, LANES)),
+        jnp.where(
+            sub == 1,
+            jnp.broadcast_to(tile_0, (ROWS, LANES)),
+            jnp.broadcast_to(tile_1, (ROWS, LANES)),
+        ),
+    )
+    own_copy = pltpu.make_async_copy(idx_own, own_sm, idx_sem.at[0])
+    own_copy.start()
+
+    for c in load_weights:
+        c.wait()
+    high, low = split(stiff_y[...])
+    w_y[...] = jnp.concatenate(
+        [jnp.concatenate([high, high], axis=1), jnp.concatenate([low, low], axis=1)], axis=0
+    )
+    high, low = split(jnp.transpose(stiff_z[...]))
+    half = jnp.concatenate([high, low], axis=1)
+    w_z[...] = jnp.concatenate([half, half], axis=0)
+
+    lax.fori_loop(reach, planes - reach, split_planes, 0, unroll=2)
+    for side in range(2):
+
+        @pl.when(s == (0 if side == 0 else ns - 1))
+        def _():
+            halo[:, 1 - side] = jnp.zeros((steps, reach) + u_a.shape[1:], BF16)
 
     half_rows = tiles_y * rows_b
     pick_b = jnp.where(iota((half_rows, rows_b), 0) % rows_b == iota((half_rows, rows_b), 1), 1.0, 0.0)

time: 66.2 us -> 65.8 us (level)
  no operation moved by 1% of the time
where the time goes in v6:
time: 65.8 us; the launch traced here: 65.7 us
  Pallas kernels  62.5 us (95%)
  local copies, waits for them, and re-layouts  1.98 us (3%)
  between operations  1.29 us (2%)
    pallas_call x1, Pallas kernels, shards(): pl.pallas_call(functools.partial(window_kernel, cfg), out_shape=(jax.Shap...  62.5 us
    unnamed x2, local copies, waits for them, and re-layouts  1.98 us

profile of v6, /device:TPU:1, one launch (start us, length us, event | category | flops | bytes accessed | tf_op | source)
XLA Modules:
  0.0 65.7 jit_solution(2622127427775842402)
XLA Ops:
  1.3 62.5 %window.1 = (f32[1,32,128,128]{3,2,1,0:T(8,128)S(1)}, f32[16,16,128]{2,1,0:T(8,128)S(1)}) custom-call(f32[1,32,128,128]{3,2,1,0:T(8,128)} %prev_hbm.1, f32[1,32,128,128]{3,2,1,0:T(8,128)} %now_hbm.1, f32[1,4,32,128,128]{4,3,2,1,0:T(8,128)} %adj_hbm.1, f32[1,32,128,128]{3,2,1,0:T(8,128)} %back_hbm.1, f32[9,1,32]{2,1,0:T(1,128)} %bitcast.2, ...), custom_call_target="tpu_custom_call" | custom-call | tf_op jit(solution)/shard_map/window/pallas_call | solution.py:720
  63.7 1.3 %copy.17 = f32[1,32,128,128]{3,2,1,0:T(8,128)} copy(f32[1,32,128,128]{3,2,1,0:T(8,128)S(1)} %get-tuple-element.4) | data formatting | bytes 4194304
  65.1 0.7 copy.18

commit v7 on v6

--- a/solution.py
+++ b/solution.py
@@ -400,7 +400,7 @@
     pairs = planes // 2
     edge = reach // 2
 
-    def over_interior(body, unroll=6):
+    def over_interior(body, unroll=12):
         def interior(i, carry):
             body(2 * i)
             return carry
@@ -532,7 +532,7 @@
             own_part(now, side)
         last = step == steps - 1
         if last:
-            over_interior(grad_pair, 4)
+            over_interior(grad_pair, 6)
         for i in range(2):
             side = (step + i) % 2
             take_halo(step, side)

time: 65.8 us -> 66.1 us (level)
  no operation moved by 1% of the time
where the time goes in v7:
time: 66.1 us; the launch traced here: 65.6 us
  Pallas kernels  62.3 us (94%)
  local copies, waits for them, and re-layouts  1.98 us (3%)
  between operations  1.29 us (2%)
    pallas_call x1, Pallas kernels, shards(): pl.pallas_call(functools.partial(window_kernel, cfg), out_shape=(jax.Shap...  62.3 us
    unnamed x2, local copies, waits for them, and re-layouts  1.98 us

profile of v7, /device:TPU:1, one launch (start us, length us, event | category | flops | bytes accessed | tf_op | source)
XLA Modules:
  0.0 65.6 jit_solution(1763804113194867043)
XLA Ops:
  1.3 62.3 %window.1 = (f32[1,32,128,128]{3,2,1,0:T(8,128)S(1)}, f32[16,16,128]{2,1,0:T(8,128)S(1)}) custom-call(f32[1,32,128,128]{3,2,1,0:T(8,128)} %prev_hbm.1, f32[1,32,128,128]{3,2,1,0:T(8,128)} %now_hbm.1, f32[1,4,32,128,128]{4,3,2,1,0:T(8,128)} %adj_hbm.1, f32[1,32,128,128]{3,2,1,0:T(8,128)} %back_hbm.1, f32[9,1,32]{2,1,0:T(1,128)} %bitcast.2, ...), custom_call_target="tpu_custom_call" | custom-call | tf_op jit(solution)/shard_map/window/pallas_call | solution.py:720
  63.6 1.3 %copy.17 = f32[1,32,128,128]{3,2,1,0:T(8,128)} copy(f32[1,32,128,128]{3,2,1,0:T(8,128)S(1)} %get-tuple-element.4) | data formatting | bytes 4194304
  64.9 0.7 copy.18
